TPU v7x, 512 devices: a whole 4x4x16 slice. The times are simulated.
512 devices in a mesh: tile: 32 (over z, core), tmpl: 16 (over y, x).
Axes of the slice: x: 4, y: 4, z: 16, core: 2. Of those that a mesh axis runs over, the one named last changes fastest.
Arguments:
- sky_image: float32 [10, 512, 2048], P(None, 'tile'), may hold values from -8 to 8
- inverse_var: float32 [10, 512, 2048], P(None, 'tile'), may hold values from 0.3 to 3
- kernel_taps: float32 [10, 17], replicated, may hold values from 0.2 to 1
- kernel_sizes: int32 [10], replicated, may hold values from 1 to 8, as said below
- templates: float32 [10, 2048], P(None, 'tmpl'), may hold values from 0.1 to 10
- grid_index: int32 [3, 2048], P(None, 'tmpl'), may hold values from 0 to 63
Outputs:
- post_means: float32 [3, 512, 2048], P(None, 'tile', 'tmpl')
- log_evidence: float32 [512, 2048], P('tile', 'tmpl')
Inputs may be any that keep to these rules, and one draw needn't show every extreme that they name: `kernel_sizes`: some band has half-width 8 and some other band has half-width 1.
All inputs are finite; a program needn't handle non-finite values.
Results may differ from a plain program's by a relative error of at most 0.0003.
Values sent between devices are 32-bit elements; how exact they have to be, the bound alone decides.
No kernel may reach another device: no remote copies, remote signals or barrier semaphores. Data moves between devices by JAX's collectives and lax.ppermute only.
A program may use at most 64 MiB of HBM per device.

v0:
```python
import math

import jax
import jax.numpy as jnp
from jax import lax
from jax.sharding import PartitionSpec as P

GRID = 64


def with_halo(x, sides, width):
    for axis, dim in sides:
        count, length = (lax.axis_size(axis), x.shape[dim])
        up = [(i, (i + 1) % count) for i in range(count - 1)]
        down = [(j, i) for i, j in up]
        last = lax.slice_in_dim(x, length - width, length, axis=dim)
        leading = lax.slice_in_dim(x, 0, width, axis=dim)
        before = lax.ppermute(last, axis, up)
        after = lax.ppermute(leading, axis, down)
        x = jnp.concatenate([before, x, after], axis=dim)
    return x


def joined_along(pieces, dim):
    pieces = jnp.moveaxis(pieces, 0, dim)
    lengths = pieces.shape
    return pieces.reshape(*lengths[:dim], lengths[dim] * lengths[dim + 1], *lengths[dim + 2 :])


def sent_to_all(x, axis):
    copies = jnp.broadcast_to(x, (lax.axis_size(axis), *x.shape))
    return lax.all_to_all(copies, axis, split_axis=0, concat_axis=0, tiled=True)


def gather_directly(x, axis, dim):
    return joined_along(sent_to_all(x, axis), dim)


def in_one_piece(arrays, axis, dim, along):
    ends, at = ([], 0)
    for a in arrays[:-1]:
        at += a.shape[along]
        ends.append(at)
    both = jnp.concatenate(arrays, axis=along)
    return tuple(jnp.split(gather_directly(both, axis, dim), ends, axis=along))


def kernel_table(kernel_taps, kernel_sizes, radius):
    offsets = jnp.arange(2 * radius + 1, dtype=jnp.int32) - radius
    inside = jnp.abs(offsets)[None, :] <= kernel_sizes[:, None]
    masked = jnp.where(inside, kernel_taps, jnp.float32(0.0))
    return masked / jnp.sum(masked, axis=1, keepdims=True)


def convolve_rows(padded, kernel, height, radius):
    result = jnp.zeros((padded.shape[0], height, padded.shape[2]), jnp.float32)
    for offset in range(2 * radius + 1):
        result = result + kernel[:, offset, None, None] * padded[:, offset : offset + height, :]
    return result


def convolve_cols(padded, kernel, width, radius):
    result = jnp.zeros((padded.shape[0], padded.shape[1], width), jnp.float32)
    for offset in range(2 * radius + 1):
        result = result + kernel[:, offset, None, None] * padded[:, :, offset : offset + width]
    return result


def fit_pixels(flux, weight, bank, coords):
    bands, pixels = flux.shape
    block = math.gcd(pixels, 2048)
    count = pixels // block
    flux_blocks = flux.reshape(bands, count, block).transpose(1, 0, 2)
    weight_blocks = weight.reshape(bands, count, block).transpose(1, 0, 2)
    squared = bank * bank

    def one_block(pair):
        flux_part, weight_part = pair
        weighted = weight_part * flux_part
        self_term = jnp.sum(weighted * flux_part, axis=0)
        cross = jnp.einsum("bp,bk->pk", weighted, bank, precision=lax.Precision.HIGHEST)
        norm_tt = jnp.einsum("bp,bk->pk", weight_part, squared, precision=lax.Precision.HIGHEST)
        loglike = -0.5 * (self_term[:, None] - cross * cross / norm_tt)
        peak = jnp.max(loglike, axis=1)
        expo = jnp.exp(loglike - peak[:, None])
        total = jnp.sum(expo, axis=1)
        moments = jnp.einsum("pk,qk->qp", expo, coords, precision=lax.Precision.HIGHEST)
        return (peak, total, moments)

    peak, total, moments = lax.map(one_block, (flux_blocks, weight_blocks))
    return (
        peak.reshape(pixels),
        total.reshape(pixels),
        moments.transpose(1, 0, 2).reshape(3, pixels),
    )


def body(sky_image, inverse_var, kernel_taps, kernel_sizes, templates, grid_index):
    radius = (kernel_taps.shape[1] - 1) // 2
    bands, height, width = sky_image.shape
    shards = lax.axis_size("tmpl")
    col_block = width // shards
    col_start = lax.axis_index("tmpl") * col_block
    kernel = kernel_table(kernel_taps, kernel_sizes, radius)
    coords = (grid_index.astype(jnp.float32) + 0.5) / GRID
    padded_cols = jnp.pad(sky_image, ((0, 0), (0, 0), (radius, radius)))
    own_cols = lax.dynamic_slice_in_dim(padded_cols, col_start, col_block + 2 * radius, 2)
    extended = with_halo(own_cols, (("tile", 1),), radius)
    smooth = convolve_rows(extended, kernel, height, radius)
    flux = convolve_cols(smooth, kernel, col_block, radius)
    own_weight = lax.dynamic_slice_in_dim(inverse_var, col_start, col_block, 2)
    full_bank, full_coords = in_one_piece((templates, coords), "tmpl", 1, 0)
    peak, total, moments = fit_pixels(
        flux.reshape(bands, height * col_block),
        own_weight.reshape(bands, height * col_block),
        full_bank,
        full_coords,
    )
    peak = peak.reshape(height, col_block)
    total = total.reshape(height, col_block)
    moments = moments.reshape(3, height, col_block)
    post_means = moments / total[None]
    log_evidence = peak + jnp.log(total)
    return (post_means, log_evidence)


def solution(mesh):
    placed = (
        P(None, "tile", None),
        P(None, "tile", None),
        P(),
        P(),
        P(None, "tmpl"),
        P(None, "tmpl"),
    )
    return jax.shard_map(
        body,
        mesh=mesh,
        in_specs=placed,
        out_specs=(P(None, "tile", "tmpl"), P("tile", "tmpl")),
        check_vma=False,
    )
```

profile of v0, /device:TPU:247, one launch (start us, length us, event | category | flops | bytes accessed | tf_op | source)
XLA Modules:
  0.0 81.6 jit_solution(13414504921352713320)
XLA Ops:
  0.6 0.7 add_multiply_fusion
  1.3 0.7 pad_maximum_fusion.2
  2.0 0.6 broadcast_in_dim.23
  2.7 6.6 %all-to-all-start = ((f32[16,13,128]{2,1,0:T(8,128)}), f32[16,13,128]{2,1,0:T(8,128)S(1)}, u32[]{:S(2)}, u32[]{:S(2)}) async-start(f32[16,13,128]{2,1,0:T(8,128)} %broadcast_in_dim.23), calls=%async_computation | async-start | bytes 262144 | tf_op jit(solution)/shard_map/all_to_all | solution.py:32
  9.3 1.1 %pad_dynamic-slice_fusion.1 = (f32[10,8,144]{2,1,0:T(8,128)S(1)}, f32[10,8,144]{2,1,0:T(8,128)S(1)}) fusion(s32[]{:T(128)S(6)} %add.174, s32[]{:T(128)S(6)} %select_n.12, f32[10,16,2048]{2,1,0:T(8,128)} %param.6), kind=kLoop, calls=%fused_computation.3 | loop fusion | bytes 1402888 | tf_op jit(solution)/shard_map/slice | solution.py:16
  10.4 5.9 %collective-permute-start = (f32[10,8,144]{2,1,0:T(8,128)S(1)}, f32[10,8,144]{2,1,0:T(8,128)S(1)}, u32[]{:S(2)}, u32[]{:S(2)}) collective-permute-start(f32[10,8,144]{2,1,0:T(8,128)S(1)} %get-tuple-element.61), channel_id=1, source_target_pairs={{0,16},{16,32},{32,48},{48,64},{64,80},{80,96},{96,112},{112,128},... | collective-permute-start | bytes 138248 | tf_op jit(solution)/shard_map/ppermute | solution.py:18
  16.3 1.9 %collective-permute-start.1 = (f32[10,8,144]{2,1,0:T(8,128)S(1)}, f32[10,8,144]{2,1,0:T(8,128)S(1)}, u32[]{:S(2)}, u32[]{:S(2)}) collective-permute-start(f32[10,8,144]{2,1,0:T(8,128)S(1)} %get-tuple-element.62), channel_id=1, source_target_pairs={{16,0},{32,16},{48,32},{64,48},{80,64},{96,80},{112,96},{128,112},... | collective-permute-start | bytes 138248 | tf_op jit(solution)/shard_map/ppermute | solution.py:19
  18.2 1.1 %pad_dynamic-slice_fusion.2 = f32[10,16,144]{2,1,0:T(8,128)S(1)} fusion(s32[]{:T(128)S(6)} %select_n.12, f32[10,16,2048]{2,1,0:T(8,128)} %param.6), kind=kLoop, calls=%fused_computation.4 | loop fusion | bytes 1402884 | tf_op jit(solution)/shard_map/dynamic_slice | solution.py:107
  19.3 0.9 %fusion.63 = f32[10]{0:T(128)S(1)} fusion(f32[10,17]{1,0:T(8,128)} %param.8, s32[17]{0:T(128)S(1)} %add_abs_fusion, s32[10]{0:T(128)} %param.9), kind=kLoop, calls=%fused_computation.138 | loop fusion | flops 500 | bytes 828 | tf_op jit(solution)/shard_map/reduce_sum | solution.py:52
  20.2 0.8 fusion.62
  21.0 0.5 slice_reduce_fusion.16
  21.5 0.0 collective-permute-done
  21.5 1.8 %collective-permute-done.1 = f32[10,8,144]{2,1,0:T(8,128)S(1)} collective-permute-done((f32[10,8,144]{2,1,0:T(8,128)S(1)}, f32[10,8,144]{2,1,0:T(8,128)S(1)}, u32[]{:S(2)}, u32[]{:S(2)}) %collective-permute-start.1) | collective-permute-done | bytes 46112 | tf_op jit(solution)/shard_map/ppermute | solution.py:19
  23.3 0.4 fusion.3
  23.7 1.5 %multiply_reduce_fusion = (f32[16,128]{1,0:T(8,128)S(1)}, f32[10,16,128]{2,1,0:T(8,128)S(1)}, f32[10,16,128]{2,1,0:T(8,128)S(1)}) fusion(f32[10,16,2048]{2,1,0:T(8,128)} %param.7, s32[]{:T(128)S(6)} %select_n.10, f32[10,16,144]{2,1,0:T(8,128)S(1)} %fusion.3, f32[10]{0:T(128)S(1)} %get-tuple-element.40, f32[10]{0:T(128)S(1)} %get-tuple-element.41, ...), kind=kLoop, calls=%fused_computation.116 | loop fusion | flops 735232 | bytes 1647276 | tf_op jit(solution)/shard_map/while/body/eval_jaxpr/reduce_sum | solution.py:80
  25.4 0.0 all-to-all-done
  25.6 13.8 %fusion.67 = f32[2048,2048]{1,0:T(8,128)S(1)} fusion(f32[10,2048]{1,0:T(8,128)S(1)} %bitcast.28, f32[10,2048]{1,0:T(8,128)S(1)} %bitcast.29), kind=kOutput, calls=%fused_computation.146 | convolution fusion | flops 503316480 | bytes 16941056 | tf_op jit(solution)/shard_map/while/body/eval_jaxpr/bp,bk->pk/dot_general | solution.py:82
  39.4 19.4 %fusion.66 = (f32[2048]{0:T(1024)S(1)}, f32[2048,2048]{1,0:T(8,128)}) fusion(f32[2048,2048]{1,0:T(8,128)S(1)} %fusion.67, f32[10,2048]{1,0:T(8,128)S(1)} %bitcast.36, f32[10,2048]{1,0:T(8,128)S(1)} %bitcast.37, f32[2048]{0:T(1024)S(1)} %bitcast.39), kind=kOutput, calls=%fused_computation.145 | convolution fusion | flops 524285952 | bytes 33734656 | tf_op jit(solution)/shard_map/while/body/eval_jaxpr/bp,bk->pk/dot_general | solution.py:81
  58.8 7.5 %fusion.64 = (f32[2048]{0:T(1024)S(1)}, f32[2048,2048]{1,0:T(8,128)S(1)}) fusion(f32[2048,2048]{1,0:T(8,128)} %get-tuple-element.66, f32[2048]{0:T(1024)S(1)} %get-tuple-element.65), kind=kLoop, calls=%fused_computation.143 | loop fusion | flops 8386560 | bytes 33570816 | tf_op jit(solution)/shard_map/while/body/eval_jaxpr/reduce_sum | solution.py:86
  66.4 0.6 bitcast_add_fusion
  67.0 14.0 %convolution_divide_fusion = f32[3,16,128]{2,0,1:T(4,128)S(1)} fusion(f32[3,2048,1]{1,0,2:T(4,128)S(1)} %reshape.45, f32[16,128,2048]{2,1,0:T(8,128)S(1)} %bitcast.27, f32[16,128]{1,0:T(8,128)S(1)} %bitcast.38), kind=kOutput, calls=%fused_computation.5 | convolution fusion | flops 151001088 | bytes 16834560 | tf_op jit(solution)/shard_map/while/body/eval_jaxpr/pk,qk->qp/dot_general | solution.py:87
  81.0 0.6 copy.15
  (13 shorter events, 0.3 us)
Async XLA Ops:
  2.7 22.7 %all-to-all-start = ((f32[16,13,128]{2,1,0:T(8,128)}), f32[16,13,128]{2,1,0:T(8,128)S(1)}, u32[]{:S(2)}, u32[]{:S(2)}) async-start(f32[16,13,128]{2,1,0:T(8,128)} %broadcast_in_dim.23), calls=%async_computation | async-start | bytes 262144 | tf_op jit(solution)/shard_map/all_to_all | solution.py:32
  10.4 11.0 %collective-permute-start = (f32[10,8,144]{2,1,0:T(8,128)S(1)}, f32[10,8,144]{2,1,0:T(8,128)S(1)}, u32[]{:S(2)}, u32[]{:S(2)}) collective-permute-start(f32[10,8,144]{2,1,0:T(8,128)S(1)} %get-tuple-element.61), channel_id=1, source_target_pairs={{0,16},{16,32},{32,48},{48,64},{64,80},{80,96},{96,112},{112,128},... | collective-permute-start | bytes 138248 | tf_op jit(solution)/shard_map/ppermute | solution.py:18
  16.3 7.0 %collective-permute-start.1 = (f32[10,8,144]{2,1,0:T(8,128)S(1)}, f32[10,8,144]{2,1,0:T(8,128)S(1)}, u32[]{:S(2)}, u32[]{:S(2)}) collective-permute-start(f32[10,8,144]{2,1,0:T(8,128)S(1)} %get-tuple-element.62), channel_id=1, source_target_pairs={{16,0},{32,16},{48,32},{64,48},{80,64},{96,80},{112,96},{128,112},... | collective-permute-start | bytes 138248 | tf_op jit(solution)/shard_map/ppermute | solution.py:19
where the time goes:
time: 82.3 us; the launch traced here: 81.6 us
  matrix products  47.2 us (57%)
  starting transfers between devices  14.4 us (17%)
  other arithmetic  13.1 us (16%)
  local copies, waits for them, and re-layouts  4.2 us (5%)
  waiting for transfers between devices  1.81 us (2%)
    dot_general x1, matrix products, one_block(): jnp.einsum('bp,bk->pk', weighted, bank, precision=lax.Precision.HIGHEST)  19.4 us
    dot_general x1, matrix products, one_block(): jnp.einsum('pk,qk->qp', expo, coords, precision=lax.Precision.HIGHEST)  14 us
    dot_general x1, matrix products, one_block(): jnp.einsum('bp,bk->pk', weight_part, squared, precision=lax.Precision.HIG...  13.8 us
    reduce_sum x1, other arithmetic, one_block(): total = jnp.sum(expo, axis=1)  7.52 us
    all_to_all x1, starting transfers between devices, sent_to_all(): return lax.all_to_all(copies, axis, split_axis=0, concat_axis=0, tiled=True)  6.64 us
    ppermute x1, starting transfers between devices, with_halo(): before = lax.ppermute(last, axis, up)  5.88 us
    ppermute x1, starting transfers between devices, with_halo(): after = lax.ppermute(leading, axis, down)  1.92 us
    ppermute x1, waiting for transfers between devices, with_halo(): after = lax.ppermute(leading, axis, down)  1.8 us
  transfers between devices with their start and end apart: 3, of which 1 were waited for; matrix products, arithmetic and copies ran while one was open for 8% of the time, Pallas kernels for 0%

commit v1 on v0

--- a/solution.py
+++ b/solution.py
@@ -1,8 +1,11 @@
+import functools
 import math
 
 import jax
 import jax.numpy as jnp
 from jax import lax
+from jax.experimental import pallas as pl
+from jax.experimental.pallas import tpu as pltpu
 from jax.sharding import PartitionSpec as P
 
 GRID = 64
@@ -66,33 +69,88 @@
     return result
 
 
-def fit_pixels(flux, weight, bank, coords):
-    bands, pixels = flux.shape
-    block = math.gcd(pixels, 2048)
-    count = pixels // block
-    flux_blocks = flux.reshape(bands, count, block).transpose(1, 0, 2)
-    weight_blocks = weight.reshape(bands, count, block).transpose(1, 0, 2)
-    squared = bank * bank
+SCALE = math.sqrt(0.5 / math.log(2.0))
+LN2 = math.log(2.0)
+BF = jnp.bfloat16
 
-    def one_block(pair):
-        flux_part, weight_part = pair
-        weighted = weight_part * flux_part
-        self_term = jnp.sum(weighted * flux_part, axis=0)
-        cross = jnp.einsum("bp,bk->pk", weighted, bank, precision=lax.Precision.HIGHEST)
-        norm_tt = jnp.einsum("bp,bk->pk", weight_part, squared, precision=lax.Precision.HIGHEST)
-        loglike = -0.5 * (self_term[:, None] - cross * cross / norm_tt)
-        peak = jnp.max(loglike, axis=1)
-        expo = jnp.exp(loglike - peak[:, None])
-        total = jnp.sum(expo, axis=1)
-        moments = jnp.einsum("pk,qk->qp", expo, coords, precision=lax.Precision.HIGHEST)
-        return (peak, total, moments)
+def split3(x):
+    a = x.astype(BF); r = x - a.astype(jnp.float32)
+    b = r.astype(BF); r = r - b.astype(jnp.float32)
+    return a, b, r.astype(BF)
 
-    peak, total, moments = lax.map(one_block, (flux_blocks, weight_blocks))
-    return (
-        peak.reshape(pixels),
-        total.reshape(pixels),
-        moments.transpose(1, 0, 2).reshape(3, pixels),
-    )
+def recip(t):
+    r = pl.reciprocal(t, approx=True)
+    return r * (2.0 - t * r)
+
+def fit_kernel(flux_ref, wt_ref, bank_ref, pm_ref, le_ref, lc, lt, cs, g_ref, *, div, nexp, KC=256):
+    zeros32 = jnp.zeros((32, 128), jnp.float32)
+    row16 = lax.broadcasted_iota(jnp.int32, (16, 128), 0)
+    for s in range(16):
+        blk = bank_ref[s]
+        T = jnp.where(row16 < 10, blk, 0.0)
+        for dst, X in ((lc, T), (lt, T * T)):
+            a, b, c = (v.astype(jnp.float32) for v in split3(X))
+            st = jnp.concatenate([a, a, b, a, b, c, zeros32], axis=0)
+            dst[pl.ds(s * 128, 128), :] = st.T.astype(BF)
+        cc = (2.0 * blk + 1.0) * (1.0 / 128.0)
+        cc = jnp.where(row16 == 13, 1.0, jnp.where((row16 >= 10) & (row16 < 13), cc, 0.0))
+        cs[:, pl.ds(s * 128, 128)] = cc.astype(BF)
+
+    def rhs(r2):
+        Fc, Ft, ffs = [], [], []
+        for j in range(2):
+            f = flux_ref[2 * r2 + j]; w = wt_ref[2 * r2 + j]
+            wf = w * f
+            ffs.append(jnp.sum(wf * f, axis=0, keepdims=True))
+            wf = wf * SCALE
+            a, b, c = split3(wf)
+            Fc.append(jnp.concatenate([a, b, a, c, b, a, jnp.zeros((32, 128), BF)], axis=0))
+            a, b, c = split3(w)
+            Ft.append(jnp.concatenate([a, b, a, c, b, a, jnp.zeros((32, 128), BF)], axis=0))
+        return jnp.concatenate(Fc, 1), jnp.concatenate(Ft, 1), jnp.concatenate(ffs, 1)
+
+    def block(r2, _):
+        Fc, Ft, ff = rhs(r2)
+        m = None
+        for ch in range(2048 // KC):
+            c = jnp.dot(lc[pl.ds(ch * KC, KC), :], Fc, preferred_element_type=jnp.float32)
+            t = jnp.dot(lt[pl.ds(ch * KC, KC), :], Ft, preferred_element_type=jnp.float32)
+            if div == "div": g = c * c / t
+            elif div == "newton":
+                r = pl.reciprocal(t, approx=True)
+                g = (c * r) * (c * (2.0 - t * r))
+            elif div == "approx": g = c * c * pl.reciprocal(t, approx=True)
+            g_ref[pl.ds(ch * KC, KC), :] = g
+            mm = jnp.max(g.reshape(KC // 8, 8, 256), axis=0)
+            m = mm if m is None else jnp.maximum(m, mm)
+        m = jnp.max(m, axis=0, keepdims=True)
+        acc = jnp.zeros((16, 256), jnp.float32)
+        for ch in range(2048 // KC):
+            e = jnp.exp2(g_ref[pl.ds(ch * KC, KC), :] - m)
+            eh = e.astype(BF)
+            acc = acc + jnp.dot(cs[:, pl.ds(ch * KC, KC)], eh, preferred_element_type=jnp.float32)
+            if nexp == 2:
+                el = (e - eh.astype(jnp.float32)).astype(BF)
+                acc = acc + jnp.dot(cs[:, pl.ds(ch * KC, KC)], el, preferred_element_type=jnp.float32)
+        tot = acc[13:14]
+        pm = acc[10:13] / tot
+        le = m * LN2 - 0.5 * ff + jnp.log(tot)
+        for j in range(2):
+            sl = slice(j * 128, j * 128 + 128)
+            for q in range(3):
+                pm_ref[q, pl.ds(2 * r2 + j, 1), :] = pm[q:q + 1, sl]
+            le_ref[pl.ds(2 * r2 + j, 1), :] = le[:, sl]
+        return 0
+    lax.fori_loop(0, 8, block, 0)
+
+def fit(flux, wt, bank, div="div", nexp=1, KC=256):
+    vm = pl.BlockSpec(memory_space=pltpu.VMEM)
+    return pl.pallas_call(
+        functools.partial(fit_kernel, div=div, nexp=nexp, KC=KC),
+        out_shape=(jax.ShapeDtypeStruct((3, 16, 128), jnp.float32), jax.ShapeDtypeStruct((16, 128), jnp.float32)),
+        in_specs=[vm, vm, vm], out_specs=(vm, vm),
+        scratch_shapes=[pltpu.VMEM((2048, 128), BF), pltpu.VMEM((2048, 128), BF), pltpu.VMEM((16, 2048), BF), pltpu.VMEM((2048, 256), jnp.float32)],
+    )(flux, wt, bank)
 
 
 def body(sky_image, inverse_var, kernel_taps, kernel_sizes, templates, grid_index):
@@ -102,26 +160,16 @@
     col_block = width // shards
     col_start = lax.axis_index("tmpl") * col_block
     kernel = kernel_table(kernel_taps, kernel_sizes, radius)
-    coords = (grid_index.astype(jnp.float32) + 0.5) / GRID
     padded_cols = jnp.pad(sky_image, ((0, 0), (0, 0), (radius, radius)))
     own_cols = lax.dynamic_slice_in_dim(padded_cols, col_start, col_block + 2 * radius, 2)
     extended = with_halo(own_cols, (("tile", 1),), radius)
     smooth = convolve_rows(extended, kernel, height, radius)
     flux = convolve_cols(smooth, kernel, col_block, radius)
     own_weight = lax.dynamic_slice_in_dim(inverse_var, col_start, col_block, 2)
-    full_bank, full_coords = in_one_piece((templates, coords), "tmpl", 1, 0)
-    peak, total, moments = fit_pixels(
-        flux.reshape(bands, height * col_block),
-        own_weight.reshape(bands, height * col_block),
-        full_bank,
-        full_coords,
-    )
-    peak = peak.reshape(height, col_block)
-    total = total.reshape(height, col_block)
-    moments = moments.reshape(3, height, col_block)
-    post_means = moments / total[None]
-    log_evidence = peak + jnp.log(total)
-    return (post_means, log_evidence)
+    bank = jnp.concatenate([templates, grid_index.astype(jnp.float32), jnp.zeros((3, templates.shape[1]), jnp.float32)], axis=0)
+    bank = sent_to_all(bank, "tmpl")
+    pad = ((0, 0), (0, 6), (0, 0))
+    return fit(jnp.pad(flux.transpose(1, 0, 2), pad), jnp.pad(own_weight.transpose(1, 0, 2), pad), bank)
 
 
 def solution(mesh):

time: 82.3 us -> 40.2 us (0.49)
  the two profiles are of different devices: /device:TPU:247 before, /device:TPU:1 now
where the time goes in v1:
time: 40.2 us; the launch traced here: 39.8 us
  starting transfers between devices  14.2 us (35%)
  Pallas kernels  12.8 us (32%)
  local copies, waits for them, and re-layouts  7.16 us (18%)
  other arithmetic  4.87 us (12%)
  between operations  0.78 us (2%)
    pallas_call x1, Pallas kernels, fit(): pl.pallas_call(functools.partial(fit_kernel, div=div, nexp=nexp, KC=KC),...  12.8 us
    ppermute x1, starting transfers between devices, with_halo(): after = lax.ppermute(leading, axis, down)  8.74 us
    add x1, other arithmetic, convolve_rows(): result + kernel[:, offset, None, None] * padded[:, offset:offset + height...  3.88 us
    all_to_all x1, starting transfers between devices, sent_to_all(): return lax.all_to_all(copies, axis, split_axis=0, concat_axis=0, tiled=True)  3.51 us
    unnamed x14, local copies, waits for them, and re-layouts  2.93 us
    ppermute x1, starting transfers between devices, with_halo(): before = lax.ppermute(last, axis, up)  1.92 us
    slice x1, local copies, waits for them, and re-layouts, with_halo(): last = lax.slice_in_dim(x, length - width, length, axis=dim)  0.86 us
    dynamic_slice x1, local copies, waits for them, and re-layouts, body(): lax.dynamic_slice_in_dim(padded_cols, col_start, col_block + 2 * radius, 2)  0.84 us
  transfers between devices with their start and end apart: 3, of which 0 were waited for; matrix products, arithmetic and copies ran while one was open for 21% of the time, Pallas kernels for 0%

profile of v1, /device:TPU:1, one launch (start us, length us, event | category | flops | bytes accessed | tf_op | source)
XLA Modules:
  0.0 39.8 jit_solution(10472051605481617629)
XLA Ops:
  0.6 0.0 copy-start
  0.7 0.0 copy-start.5
  0.7 0.0 copy-start.3
  0.7 2.2 %copy.10 = f32[10,16,2048]{2,0,1:T(8,128)S(1)} copy(f32[10,16,2048]{2,1,0:T(8,128)} %param.6) | data formatting | bytes 2621440 | tf_op args[0]
  2.9 0.0 copy-start.2
  2.9 0.0 copy-start.4
  2.9 0.9 %pad_dynamic-slice_fusion.1 = (f32[10,8,144]{2,0,1:T(8,128)}, f32[10,8,144]{2,0,1:T(8,128)}) fusion(s32[]{:T(128)S(6)} %add.164, s32[]{:T(128)S(6)} %select_n.11, f32[10,16,2048]{2,0,1:T(8,128)S(1)} %copy.10), kind=kLoop, calls=%fused_computation.1 | loop fusion | bytes 1402888 | tf_op jit(solution)/shard_map/slice | solution.py:19
  3.8 8.7 %collective-permute-start.1 = (f32[10,8,144]{2,0,1:T(8,128)}, f32[10,8,144]{2,0,1:T(8,128)}, u32[]{:S(2)}, u32[]{:S(2)}) collective-permute-start(f32[10,8,144]{2,0,1:T(8,128)} %get-tuple-element.20), channel_id=1, source_target_pairs={{16,0},{32,16},{48,32},{64,48},{80,64},{96,80},{112,96},{128,112},... | collective-permute-start | bytes 138248 | tf_op jit(solution)/shard_map/ppermute | solution.py:22
  12.5 1.9 %collective-permute-start = (f32[10,8,144]{2,0,1:T(8,128)}, f32[10,8,144]{2,0,1:T(8,128)}, u32[]{:S(2)}, u32[]{:S(2)}) collective-permute-start(f32[10,8,144]{2,0,1:T(8,128)} %get-tuple-element.19), channel_id=1, source_target_pairs={{0,16},{16,32},{32,48},{48,64},{64,80},{80,96},{96,112},{112,128},... | collective-permute-start | bytes 138248 | tf_op jit(solution)/shard_map/ppermute | solution.py:21
  14.4 0.0 copy-done.5
  14.5 0.1 pad.16.clone
  14.6 0.0 copy-done.3
  14.6 0.1 maximum_maximum_fusion
  14.6 0.7 %broadcast_in_dim.15 = f32[16,16,128]{2,1,0:T(8,128)} broadcast(f32[16,128]{1,0:T(8,128)S(1)} %maximum_maximum_fusion), dimensions={1,2} | broadcast | bytes 139264 | tf_op jit(solution)/shard_map/broadcast_in_dim | solution.py:34
  15.3 3.5 %all-to-all-start = ((f32[16,16,128]{2,1,0:T(8,128)}), f32[16,16,128]{2,1,0:T(8,128)S(1)}, u32[]{:S(2)}, u32[]{:S(2)}) async-start(f32[16,16,128]{2,1,0:T(8,128)} %broadcast_in_dim.15), calls=%async_computation | async-start | bytes 262144 | tf_op jit(solution)/shard_map/all_to_all | solution.py:35
  18.8 0.8 %pad_dynamic-slice_fusion.2 = f32[10,16,144]{2,0,1:T(8,128)} fusion(s32[]{:T(128)S(6)} %select_n.11, f32[10,16,2048]{2,0,1:T(8,128)S(1)} %copy.10), kind=kLoop, calls=%fused_computation.2 | loop fusion | bytes 1402884 | tf_op jit(solution)/shard_map/dynamic_slice | solution.py:164
  19.7 0.0 copy-done.2
  19.7 0.0 copy-done.4
  19.7 0.2 fusion.64
  19.8 0.1 fusion.63
  19.9 0.0 copy-done
  20.0 0.5 %slice_reduce_fusion.16 = (f32[10]{0:T(128)S(1)}, f32[10]{0:T(128)S(1)}, f32[10]{0:T(128)S(1)}, f32[10]{0:T(128)S(1)}, f32[10]{0:T(128)S(1)}, /*index=5*/f32[10]...) fusion(f32[10,17]{1,0:T(8,128)S(1)} %fusion.63), kind=kLoop, calls=%fused_computation.130 | loop fusion | bytes 1360 | tf_op jit(solution)/shard_map/slice | solution.py:68
  20.5 0.7 %pad.13.wt_ref = f32[16,16,128]{2,1,0:T(8,128)} pad(f32[16,10,128]{2,1,0:T(8,128)S(1)} %bitcast.5, f32[]{:T(128)} %constant.8.clone.1), padding=0_0x0_6x0_0 | pad | bytes 212996 | tf_op jit(solution)/shard_map/jit(_pad)/pad | solution.py:172
  21.1 0.0 collective-permute-done.1
  21.1 0.0 collective-permute-done
  21.1 3.9 %fusion.3 = f32[10,16,144]{2,0,1:T(8,128)S(1)} fusion(f32[10,16,144]{2,0,1:T(8,128)} %pad_dynamic-slice_fusion.2, f32[10,8,144]{2,0,1:T(8,128)} %collective-permute-done.1, f32[10,8,144]{2,0,1:T(8,128)} %collective-permute-done, f32[10]{0:T(128)S(1)} %get-tuple-element.3, f32[10]{0:T(128)S(1)} %get-tuple-element.4, f32[10]{0:T(128)S(1)} %get-tuple-element.5, ...), kind=kLoop, calls=%fused_computation.34 | loop fusion | flops 1128960 | bytes 277160 | tf_op jit(solution)/shard_map/add | solution.py:61
  25.0 0.6 %fusion.47 = f32[16,10,128]{2,1,0:T(8,128)S(1)} fusion(f32[10,16,144]{2,0,1:T(8,128)S(1)} %fusion.3, f32[10]{0:T(128)S(1)} %get-tuple-element.3, f32[10]{0:T(128)S(1)} %get-tuple-element.4, f32[10]{0:T(128)S(1)} %get-tuple-element.5, f32[10]{0:T(128)S(1)} %get-tuple-element.6, f32[10]{0:T(128)S(1)} %get-tuple-element.7, f32[10]{0:T(128)S(1)} %get-tuple-element.8, ...), kind=kLoop, calls=%fused_computation.81 | loop fusion | flops 675840 | bytes 1475240 | tf_op jit(solution)/shard_map/transpose | solution.py:172
  25.7 0.6 %pad.12.flux_ref = f32[16,16,128]{2,1,0:T(8,128)} pad(f32[16,10,128]{2,1,0:T(8,128)S(1)} %fusion.47, f32[]{:T(128)} %constant.8.clone.1), padding=0_0x0_6x0_0 | pad | bytes 212996 | tf_op jit(solution)/shard_map/jit(_pad)/pad | solution.py:172
  26.3 0.0 all-to-all-done.bank_ref
  26.3 0.0 copy-start.1
  26.3 0.7 %copy-done.1 = f32[16,16,128]{2,1,0:T(8,128)} copy-done((f32[16,16,128]{2,1,0:T(8,128)}, f32[16,16,128]{2,1,0:T(8,128)S(1)}, u32[]{:S(2)}) %copy-start.1) | copy-done | bytes 131096
  27.0 12.8 %shard_map.77 = (f32[3,16,128]{2,1,0:T(8,128)}, f32[16,128]{1,0:T(8,128)}) custom-call(f32[16,16,128]{2,1,0:T(8,128)} %pad.12.flux_ref, f32[16,16,128]{2,1,0:T(8,128)} %pad.13.wt_ref, f32[16,16,128]{2,1,0:T(8,128)} %copy-done.1), custom_call_target="tpu_custom_call" | custom-call | tf_op jit(solution)/shard_map/pallas_call | solution.py:148
  (5 shorter events, 0.1 us)
Async XLA Ops:
  0.6 19.3 %copy-start = (f32[10,16,2048]{2,1,0:T(8,128)S(1)}, f32[10,16,2048]{2,1,0:T(8,128)}, u32[]{:S(2)}) copy-start(f32[10,16,2048]{2,1,0:T(8,128)} %param.7) | copy-start | bytes 3932164
  0.7 13.8 %copy-start.5 = (s32[3,128]{1,0:T(4,128)S(1)}, s32[3,128]{1,0:T(4,128)}, u32[]{:S(2)}) copy-start(s32[3,128]{1,0:T(4,128)} %param.11) | copy-start | bytes 4612
  0.7 13.9 %copy-start.3 = (f32[10,128]{1,0:T(8,128)S(1)}, f32[10,128]{1,0:T(8,128)}, u32[]{:S(2)}) copy-start(f32[10,128]{1,0:T(8,128)} %param.10) | copy-start | bytes 15364
  2.9 16.8 %copy-start.2 = (f32[10,17]{1,0:T(8,128)S(1)}, f32[10,17]{1,0:T(8,128)}, u32[]{:S(2)}) copy-start(f32[10,17]{1,0:T(8,128)} %param.8) | copy-start | bytes 2044
  2.9 16.8 %copy-start.4 = (s32[10]{0:T(128)S(1)}, s32[10]{0:T(128)}, u32[]{:S(2)}) copy-start(s32[10]{0:T(128)} %param.9) | copy-start | bytes 124
  3.8 17.4 %collective-permute-start.1 = (f32[10,8,144]{2,0,1:T(8,128)}, f32[10,8,144]{2,0,1:T(8,128)}, u32[]{:S(2)}, u32[]{:S(2)}) collective-permute-start(f32[10,8,144]{2,0,1:T(8,128)} %get-tuple-element.20), channel_id=1, source_target_pairs={{16,0},{32,16},{48,32},{64,48},{80,64},{96,80},{112,96},{128,112},... | collective-permute-start | bytes 138248 | tf_op jit(solution)/shard_map/ppermute | solution.py:22
  12.5 8.6 %collective-permute-start = (f32[10,8,144]{2,0,1:T(8,128)}, f32[10,8,144]{2,0,1:T(8,128)}, u32[]{:S(2)}, u32[]{:S(2)}) collective-permute-start(f32[10,8,144]{2,0,1:T(8,128)} %get-tuple-element.19), channel_id=1, source_target_pairs={{0,16},{16,32},{32,48},{48,64},{64,80},{80,96},{96,112},{112,128},... | collective-permute-start | bytes 138248 | tf_op jit(solution)/shard_map/ppermute | solution.py:21
  15.3 11.0 %all-to-all-start = ((f32[16,16,128]{2,1,0:T(8,128)}), f32[16,16,128]{2,1,0:T(8,128)S(1)}, u32[]{:S(2)}, u32[]{:S(2)}) async-start(f32[16,16,128]{2,1,0:T(8,128)} %broadcast_in_dim.15), calls=%async_computation | async-start | bytes 262144 | tf_op jit(solution)/shard_map/all_to_all | solution.py:35
  26.3 0.7 %copy-start.1 = (f32[16,16,128]{2,1,0:T(8,128)}, f32[16,16,128]{2,1,0:T(8,128)S(1)}, u32[]{:S(2)}) copy-start(f32[16,16,128]{2,1,0:T(8,128)S(1)} %all-to-all-done.bank_ref) | copy-start | bytes 393220

commit v2 on v1

v2 whole, which is shorter than its diff:
```python
import functools
import math

import jax
import jax.numpy as jnp
from jax import lax
from jax.experimental import pallas as pl
from jax.experimental.pallas import tpu as pltpu
from jax.sharding import PartitionSpec as P

BANDS = 10
RADIUS = 8
TAPS = 2 * RADIUS + 1
LANES = 128
SUB = 16
SCALE = math.sqrt(0.5 / math.log(2.0))
LN2 = math.log(2.0)
BF = jnp.bfloat16
F32 = jnp.float32


def prep_kernel(sky, ivar, taps, sizes, templates, grid_index, bank, first, last, weight, cols, tm, gi, tp, sz, sems):
    c = lax.axis_index("tmpl")
    shards = bank.shape[0]
    at = lambda i: pl.ds(pl.multiple_of(i * LANES, LANES), LANES)
    copies = [
        pltpu.make_async_copy(sky.at[:, :, at(jnp.maximum(c - 1, 0))], cols.at[0], sems.at[0]),
        pltpu.make_async_copy(sky.at[:, :, at(c)], cols.at[1], sems.at[1]),
        pltpu.make_async_copy(sky.at[:, :, at(jnp.minimum(c + 1, shards - 1))], cols.at[2], sems.at[2]),
        pltpu.make_async_copy(taps, tp, sems.at[3]),
        pltpu.make_async_copy(sizes, sz, sems.at[4]),
        pltpu.make_async_copy(templates, tm, sems.at[5]),
        pltpu.make_async_copy(grid_index, gi, sems.at[6]),
        pltpu.make_async_copy(ivar.at[:, :, at(c)], weight, sems.at[7]),
    ]
    for copy in copies:
        copy.start()
    copies[5].wait()
    copies[6].wait()
    rows = jnp.concatenate([tm[...], gi[...].astype(F32), jnp.zeros((SUB - BANDS - 3, LANES), F32)], axis=0)
    for s in range(shards):
        bank[s] = rows
    for copy in copies[:5]:
        copy.wait()
    lane = lax.broadcasted_iota(jnp.int32, (16, LANES), 1)
    right_ok = jnp.where(c < shards - 1, 1.0, 0.0)
    left_ok = jnp.where(c > 0, 1.0, 0.0)
    for b in range(BANDS):
        main = cols[1, b]
        side = jnp.where(lane < LANES // 2, cols[2, b] * right_ok, cols[0, b] * left_ok)
        size = sz[b]
        acc = main * tp[b, RADIUS]
        for d in range(1, RADIUS + 1):
            up = pltpu.roll(jnp.where(lane >= d, main, side), LANES - d, 1)
            down = pltpu.roll(jnp.where(lane < LANES - d, main, side), d, 1)
            acc = acc + up * jnp.where(d <= size, tp[b, RADIUS + d], 0.0)
            acc = acc + down * jnp.where(d <= size, tp[b, RADIUS - d], 0.0)
        first[pl.ds(b, 8, stride=BANDS), :] = acc[:8]
        last[pl.ds(b, 8, stride=BANDS), :] = acc[8:]
    copies[7].wait()


def prep(sky, ivar, taps, sizes, templates, grid_index, shards):
    hbm = pl.BlockSpec(memory_space=pl.ANY)
    vm = pl.BlockSpec(memory_space=pltpu.VMEM)
    halo = pltpu.VMEM((8 * BANDS, LANES), F32)
    return pl.pallas_call(
        prep_kernel,
        out_shape=(pltpu.VMEM((shards, SUB, LANES), F32), halo, halo, pltpu.VMEM((BANDS, 16, LANES), F32)),
        in_specs=[hbm] * 6,
        out_specs=(vm,) * 4,
        scratch_shapes=[
            pltpu.VMEM((3, BANDS, 16, LANES), F32),
            pltpu.VMEM((BANDS, LANES), F32),
            pltpu.VMEM((3, LANES), jnp.int32),
            pltpu.SMEM((BANDS, TAPS), F32),
            pltpu.SMEM((BANDS,), jnp.int32),
            pltpu.SemaphoreType.DMA((8,)),
        ],
        name="prep",
    )(sky, ivar, taps, sizes, templates, grid_index)


def split3(x):
    a = x.astype(BF)
    r = x - a.astype(F32)
    b = r.astype(BF)
    r = r - b.astype(F32)
    return a, b, r.astype(BF)


def fit_kernel(up, first, last, down, wt, taps, sizes, bank, pm_ref, le_ref, ext, flux, tk, lc, lt, cs, g_ref, e_ref, *, KC):
    row16 = lax.broadcasted_iota(jnp.int32, (SUB, LANES), 0)
    lane16 = lax.broadcasted_iota(jnp.int32, (SUB, LANES), 1)

    pad6 = jnp.zeros((SUB - BANDS, LANES), F32)
    for q, part in enumerate((up, first, last, down)):
        for r in range(8):
            ext[q * 8 + r] = jnp.concatenate([part[pl.ds(r * BANDS, BANDS), :], pad6], axis=0)
    tk[...] = jnp.zeros((SUB, LANES), F32)
    tk[0:BANDS, 0:TAPS] = taps[...]
    sv = jnp.zeros((SUB, LANES), jnp.int32)
    for b in range(BANDS):
        sv = jnp.where(row16 == b, sizes[b], sv)
    kern = jnp.where((jnp.abs(lane16 - RADIUS) <= sv) & (lane16 < TAPS) & (row16 < BANDS), tk[...], 0.0)
    norm = jnp.sum(kern, axis=1, keepdims=True)
    norm = jnp.where(row16 < BANDS, jnp.broadcast_to(norm, (SUB, LANES)), 1.0)
    kern = kern / (norm * norm)
    kv = [jnp.broadcast_to(kern[:, t : t + 1], (SUB, LANES)) for t in range(TAPS)]
    for r in range(16):
        acc = kv[0] * ext[r]
        for t in range(1, TAPS):
            acc = acc + kv[t] * ext[r + t]
        flux[r] = acc

    def lhs_prep(s):
        zeros32 = jnp.zeros((32, LANES), F32)
        blk = bank[s]
        T = jnp.where(row16 < BANDS, blk, 0.0)
        for dst, X in ((lc, T), (lt, T * T)):
            a, b, c = (v.astype(F32) for v in split3(X))
            st = jnp.concatenate([a, a, b, a, b, c, zeros32], axis=0)
            dst[pl.ds(s * LANES, LANES), :] = st.T.astype(BF)
        cc = (2.0 * blk + 1.0) * (1.0 / 128.0)
        cc = jnp.where(row16 == 13, 1.0, jnp.where((row16 >= 10) & (row16 < 13), cc, 0.0))
        cs[:, pl.ds(s * LANES, LANES)] = cc.astype(BF)

    def rhs(r2):
        Fc, Ft, ffs = [], [], []
        for j in range(2):
            f = flux[2 * r2 + j]
            w = jnp.concatenate([wt[pl.ds(2 * r2 + j, BANDS, stride=16), :], pad6], axis=0)
            wf = w * f
            ffs.append(jnp.sum(wf * f, axis=0, keepdims=True))
            z = jnp.zeros((32, LANES), BF)
            a, b, c = split3(wf * SCALE)
            Fc.append(jnp.concatenate([a, b, a, c, b, a, z], axis=0))
            a, b, c = split3(w)
            Ft.append(jnp.concatenate([a, b, a, c, b, a, z], axis=0))
        return jnp.concatenate(Fc, 1), jnp.concatenate(Ft, 1), jnp.concatenate(ffs, 1)

    NT = lc.shape[0]
    n1 = NT // KC

    def phase1(ch, Fc, Ft, m):
        c = jnp.dot(lc[pl.ds(ch * KC, KC), :], Fc, preferred_element_type=F32)
        t = jnp.dot(lt[pl.ds(ch * KC, KC), :], Ft, preferred_element_type=F32)
        g = c * c / t
        g_ref[pl.ds(ch * KC, KC), :] = g
        mm = jnp.max(g.reshape(KC // 8, 8, 256), axis=0)
        return mm if m is None else jnp.maximum(m, mm)

    def exps(k, m):
        e_ref[pl.ds(k * KC, KC), :] = jnp.exp2(g_ref[pl.ds(k * KC, KC), :] - m).astype(BF)

    def edot(k, acc):
        d = jnp.dot(cs[:, pl.ds(k * KC, KC)], e_ref[pl.ds(k * KC, KC), :], preferred_element_type=F32)
        return d if acc is None else acc + d

    def finish(r2, m, ff, acc):
        tot = acc[13:14]
        pm = acc[10:13] / tot
        le = m * LN2 - 0.5 * ff + jnp.log(tot)
        for j in range(2):
            sl = slice(j * LANES, j * LANES + LANES)
            for q in range(3):
                pm_ref[q, pl.ds(2 * r2 + j, 1), :] = pm[q : q + 1, sl]
            le_ref[pl.ds(2 * r2 + j, 1), :] = le[:, sl]

    Fc, Ft, ff0 = rhs(0)
    m = None
    for ch in range(n1):
        for s in range(ch * KC // LANES, (ch + 1) * KC // LANES):
            lhs_prep(s)
        m = phase1(ch, Fc, Ft, m)
    m0 = jnp.max(m, axis=0, keepdims=True)

    def body(i, carry):
        mp, ffp = carry
        Fc, Ft, ff = rhs(i)
        m = acc = None
        for ch in range(n1):
            if ch >= 1:
                acc = edot(ch - 1, acc)
            exps(ch, mp)
            m = phase1(ch, Fc, Ft, m)
        acc = edot(n1 - 1, acc)
        finish(i - 1, mp, ffp, acc)
        return jnp.max(m, axis=0, keepdims=True), ff

    mp, ffp = lax.fori_loop(1, 8, body, (m0, ff0))
    acc = None
    for k in range(n1):
        exps(k, mp)
        acc = edot(k, acc)
    finish(7, mp, ffp, acc)


def fit(up, first, last, down, wt, taps, sizes, bank, KC=256):
    vm = pl.BlockSpec(memory_space=pltpu.VMEM)
    sm = pl.BlockSpec(memory_space=pltpu.SMEM)
    nt = bank.shape[0] * LANES
    on_chip = lambda x: pltpu.with_memory_space_constraint(x, pltpu.VMEM)
    return pl.pallas_call(
        functools.partial(fit_kernel, KC=KC),
        out_shape=(jax.ShapeDtypeStruct((3, 16, LANES), F32), jax.ShapeDtypeStruct((16, LANES), F32)),
        in_specs=[vm, vm, vm, vm, vm, vm, sm, vm],
        out_specs=(vm, vm),
        scratch_shapes=[
            pltpu.VMEM((32, SUB, LANES), F32),
            pltpu.VMEM((16, SUB, LANES), F32),
            pltpu.VMEM((SUB, LANES), F32),
            pltpu.VMEM((nt, LANES), BF),
            pltpu.VMEM((nt, LANES), BF),
            pltpu.VMEM((SUB, nt), BF),
            pltpu.VMEM((nt, 256), F32),
            pltpu.VMEM((nt, 256), BF),
        ],
        name="fit",
    )(on_chip(up), on_chip(first), on_chip(last), on_chip(down), on_chip(wt.reshape(BANDS * 16, LANES)), taps, sizes, on_chip(bank))


def body(sky_image, inverse_var, kernel_taps, kernel_sizes, templates, grid_index):
    shards = lax.axis_size("tmpl")
    tiles = lax.axis_size("tile")
    bank, first, last, weight = prep(sky_image, inverse_var, kernel_taps, kernel_sizes, templates, grid_index, shards)
    bank = lax.all_to_all(bank, "tmpl", split_axis=0, concat_axis=0, tiled=True)
    ups = [(i, i + 1) for i in range(tiles - 1)]
    before = lax.ppermute(last, "tile", ups)
    after = lax.ppermute(first, "tile", [(j, i) for i, j in ups])
    return fit(before, first, last, after, weight, kernel_taps, kernel_sizes, bank)


def solution(mesh):
    placed = (
        P(None, "tile", None),
        P(None, "tile", None),
        P(),
        P(),
        P(None, "tmpl"),
        P(None, "tmpl"),
    )
    return jax.shard_map(
        body,
        mesh=mesh,
        in_specs=placed,
        out_specs=(P(None, "tile", "tmpl"), P("tile", "tmpl")),
        check_vma=False,
    )
```

time: 40.2 us -> 30.8 us (0.77)
  the two profiles are of different devices: /device:TPU:1 before, /device:TPU:227 now
where the time goes in v2:
time: 30.8 us; the launch traced here: 30.5 us
  starting transfers between devices  14.7 us (48%)
  Pallas kernels  10.5 us (34%)
  waiting for transfers between devices  4.6 us (15%)
  between operations  0.66 us (2%)
    pallas_call x1, Pallas kernels, fit(): pl.pallas_call(functools.partial(fit_kernel, KC=KC), out_shape=(jax.Shape...  8.4 us
    all_to_all x1, starting transfers between devices, body(): bank = lax.all_to_all(bank, 'tmpl', split_axis=0, concat_axis=0, tiled=True)  6.93 us
    ppermute x1, starting transfers between devices, body(): before = lax.ppermute(last, 'tile', ups)  5.86 us
    ppermute x1, waiting for transfers between devices, body(): after = lax.ppermute(first, 'tile', [(j, i) for i, j in ups])  4.59 us
    pallas_call x1, Pallas kernels, prep(): pl.pallas_call(prep_kernel, out_shape=(pltpu.VMEM((shards, SUB, LANES), F...  2.13 us
    ppermute x1, starting transfers between devices, body(): after = lax.ppermute(first, 'tile', [(j, i) for i, j in ups])  1.92 us
  transfers between devices with their start and end apart: 3, of which 1 were waited for; matrix products, arithmetic and copies ran while one was open for 0% of the time, Pallas kernels for 0%

profile of v2, /device:TPU:227, one launch (start us, length us, event | category | flops | bytes accessed | tf_op | source)
XLA Modules:
  0.0 30.5 jit_solution(2774884963701471936)
XLA Ops:
  0.6 2.1 %prep.1 = (f32[16,16,128]{2,1,0:T(8,128)}, f32[80,128]{1,0:T(8,128)S(1)}, f32[80,128]{1,0:T(8,128)S(1)}, f32[10,16,128]{2,1,0:T(8,128)S(1)}) custom-call(f32[10,16,2048]{2,1,0:T(8,128)} %sky.1, f32[10,16,2048]{2,1,0:T(8,128)} %ivar.1, f32[10,17]{1,0:T(8,128)} %taps.3, s32[10]{0:T(128)} %sizes.3, f32[10,128]{1,0:T(8,128)} %templates.1, s32[3,128]{1,0:T(4,128)} %grid_index.1), custom_call_target="tpu_custom_call" | custom-call | tf_op jit(solution)/shard_map/prep/pallas_call | solution.py:67
  2.8 6.9 %all-to-all-start = ((f32[16,16,128]{2,1,0:T(8,128)}), f32[16,16,128]{2,1,0:T(8,128)S(1)}, u32[]{:S(2)}, u32[]{:S(2)}) async-start(f32[16,16,128]{2,1,0:T(8,128)} %get-tuple-element.9), calls=%async_computation | async-start | bytes 262144 | tf_op jit(solution)/shard_map/all_to_all | solution.py:227
  9.7 5.9 %collective-permute-start = (f32[80,128]{1,0:T(8,128)S(1)}, f32[80,128]{1,0:T(8,128)S(1)}, u32[]{:S(2)}, u32[]{:S(2)}) collective-permute-start(f32[80,128]{1,0:T(8,128)S(1)} %get-tuple-element.6.last), channel_id=1, source_target_pairs={{0,16},{16,32},{32,48},{48,64},{64,80},{80,96},{96,112},{112,128},... | collective-permute-start | bytes 122888 | tf_op jit(solution)/shard_map/ppermute | solution.py:229
  15.6 1.9 %collective-permute-start.1 = (f32[80,128]{1,0:T(8,128)S(1)}, f32[80,128]{1,0:T(8,128)S(1)}, u32[]{:S(2)}, u32[]{:S(2)}) collective-permute-start(f32[80,128]{1,0:T(8,128)S(1)} %get-tuple-element.7.first), channel_id=1, source_target_pairs={{16,0},{32,16},{48,32},{64,48},{80,64},{96,80},{112,96},{128,112},... | collective-permute-start | bytes 122888 | tf_op jit(solution)/shard_map/ppermute | solution.py:230
  17.5 0.0 collective-permute-done.up
  17.5 4.6 %collective-permute-done.1.down = f32[80,128]{1,0:T(8,128)S(1)} collective-permute-done((f32[80,128]{1,0:T(8,128)S(1)}, f32[80,128]{1,0:T(8,128)S(1)}, u32[]{:S(2)}, u32[]{:S(2)}) %collective-permute-start.1) | collective-permute-done | bytes 40992 | tf_op jit(solution)/shard_map/ppermute | solution.py:230
  22.1 0.0 all-to-all-done.bank
  22.1 8.4 %fit.1 = (f32[3,16,128]{2,1,0:T(8,128)}, f32[16,128]{1,0:T(8,128)}) custom-call(f32[80,128]{1,0:T(8,128)S(1)} %collective-permute-done.up, f32[80,128]{1,0:T(8,128)S(1)} %get-tuple-element.7.first, f32[80,128]{1,0:T(8,128)S(1)} %get-tuple-element.6.last, f32[80,128]{1,0:T(8,128)S(1)} %collective-permute-done.1.down, f32[160,128]{1,0:T(8,128)S(1)} %bitcast.1, ...), custom_call_target="tpu_custom_call" | custom-call | tf_op jit(solution)/shard_map/fit/pallas_call | solution.py:204
Async XLA Ops:
  2.8 19.3 %all-to-all-start = ((f32[16,16,128]{2,1,0:T(8,128)}), f32[16,16,128]{2,1,0:T(8,128)S(1)}, u32[]{:S(2)}, u32[]{:S(2)}) async-start(f32[16,16,128]{2,1,0:T(8,128)} %get-tuple-element.9), calls=%async_computation | async-start | bytes 262144 | tf_op jit(solution)/shard_map/all_to_all | solution.py:227
  9.7 7.8 %collective-permute-start = (f32[80,128]{1,0:T(8,128)S(1)}, f32[80,128]{1,0:T(8,128)S(1)}, u32[]{:S(2)}, u32[]{:S(2)}) collective-permute-start(f32[80,128]{1,0:T(8,128)S(1)} %get-tuple-element.6.last), channel_id=1, source_target_pairs={{0,16},{16,32},{32,48},{48,64},{64,80},{80,96},{96,112},{112,128},... | collective-permute-start | bytes 122888 | tf_op jit(solution)/shard_map/ppermute | solution.py:229
  15.6 6.5 %collective-permute-start.1 = (f32[80,128]{1,0:T(8,128)S(1)}, f32[80,128]{1,0:T(8,128)S(1)}, u32[]{:S(2)}, u32[]{:S(2)}) collective-permute-start(f32[80,128]{1,0:T(8,128)S(1)} %get-tuple-element.7.first), channel_id=1, source_target_pairs={{16,0},{32,16},{48,32},{64,48},{80,64},{96,80},{112,96},{128,112},... | collective-permute-start | bytes 122888 | tf_op jit(solution)/shard_map/ppermute | solution.py:230

commit v3 on v2

v3 whole, which is shorter than its diff:
```python
import functools
import math

import jax
import jax.numpy as jnp
from jax import lax
from jax.experimental import pallas as pl
from jax.experimental.pallas import tpu as pltpu
from jax.sharding import PartitionSpec as P

BANDS = 10
RADIUS = 8
TAPS = 2 * RADIUS + 1
LANES = 128
SUB = 16
SCALE = math.sqrt(0.5 / math.log(2.0))
LN2 = math.log(2.0)
BF = jnp.bfloat16
F32 = jnp.float32


def bank_kernel(templates, grid_index, bank, rows, gi, sems):
    shards = bank.shape[0]
    reads = [
        pltpu.make_async_copy(templates, rows.at[0:BANDS], sems.at[0]),
        pltpu.make_async_copy(grid_index, gi, sems.at[1]),
    ]
    for copy in reads:
        copy.start()
    for copy in reads:
        copy.wait()
    rows[BANDS : BANDS + 3] = gi[...].astype(F32)
    rows[BANDS + 3 : SUB] = jnp.zeros((SUB - BANDS - 3, LANES), F32)
    writes = [pltpu.make_async_copy(rows, bank.at[s], sems.at[2 + s]) for s in range(shards)]
    for copy in writes:
        copy.start()
    for copy in writes:
        copy.wait()


def bank_copies(templates, grid_index, shards):
    hbm = pl.BlockSpec(memory_space=pl.ANY)
    return pl.pallas_call(
        bank_kernel,
        out_shape=jax.ShapeDtypeStruct((shards, SUB, LANES), F32),
        in_specs=[hbm] * 2,
        out_specs=hbm,
        scratch_shapes=[
            pltpu.VMEM((SUB, LANES), F32),
            pltpu.VMEM((3, LANES), jnp.int32),
            pltpu.SemaphoreType.DMA((2 + shards,)),
        ],
        name="bank",
    )(templates, grid_index)


def prep_kernel(sky, ivar, taps, sizes, far, near, weight, cols, tp, sz, sems, *, shards):
    c = lax.axis_index("tmpl")
    odd = lax.rem(lax.axis_index("tile"), 2) == 1
    at = lambda i: pl.ds(pl.multiple_of(i * LANES, LANES), LANES)
    copies = [
        pltpu.make_async_copy(sky.at[:, :, at(jnp.maximum(c - 1, 0))], cols.at[0], sems.at[0]),
        pltpu.make_async_copy(sky.at[:, :, at(c)], cols.at[1], sems.at[1]),
        pltpu.make_async_copy(sky.at[:, :, at(jnp.minimum(c + 1, shards - 1))], cols.at[2], sems.at[2]),
        pltpu.make_async_copy(taps, tp, sems.at[3]),
        pltpu.make_async_copy(sizes, sz, sems.at[4]),
        pltpu.make_async_copy(ivar.at[:, :, at(c)], weight, sems.at[5]),
    ]
    for copy in copies:
        copy.start()
    for copy in copies[:5]:
        copy.wait()
    lane = lax.broadcasted_iota(jnp.int32, (16, LANES), 1)
    right_ok = jnp.where(c < shards - 1, 1.0, 0.0)
    left_ok = jnp.where(c > 0, 1.0, 0.0)
    for b in range(BANDS):
        main = cols[1, b]
        side = jnp.where(lane < LANES // 2, cols[2, b] * right_ok, cols[0, b] * left_ok)
        size = sz[b]
        acc = main * tp[b, RADIUS]
        for d in range(1, RADIUS + 1):
            up = pltpu.roll(jnp.where(lane >= d, main, side), LANES - d, 1)
            down = pltpu.roll(jnp.where(lane < LANES - d, main, side), d, 1)
            acc = acc + up * jnp.where(d <= size, tp[b, RADIUS + d], 0.0)
            acc = acc + down * jnp.where(d <= size, tp[b, RADIUS - d], 0.0)
        near[pl.ds(b, 8, stride=BANDS), :] = jnp.where(odd, acc[:8], acc[8:])
        far[pl.ds(b, 8, stride=BANDS), :] = jnp.where(odd, acc[8:], acc[:8])
    copies[5].wait()


def prep(sky, ivar, taps, sizes, shards):
    hbm = pl.BlockSpec(memory_space=pl.ANY)
    vm = pl.BlockSpec(memory_space=pltpu.VMEM)
    halo = pltpu.VMEM((8 * BANDS, LANES), F32)
    return pl.pallas_call(
        functools.partial(prep_kernel, shards=shards),
        out_shape=(halo, halo, pltpu.VMEM((BANDS, 16, LANES), F32)),
        in_specs=[hbm] * 4,
        out_specs=(vm,) * 3,
        scratch_shapes=[
            pltpu.VMEM((3, BANDS, 16, LANES), F32),
            pltpu.SMEM((BANDS, TAPS), F32),
            pltpu.SMEM((BANDS,), jnp.int32),
            pltpu.SemaphoreType.DMA((6,)),
        ],
        name="prep",
    )(sky, ivar, taps, sizes)


def split3(x):
    a = x.astype(BF)
    r = x - a.astype(F32)
    b = r.astype(BF)
    r = r - b.astype(F32)
    return a, b, r.astype(BF)


def rows_kernel(got_far, got_near, far, near, wt, taps, sizes, fc_ref, ft_ref, ff_ref, ext, tk):
    row16 = lax.broadcasted_iota(jnp.int32, (SUB, LANES), 0)
    lane16 = lax.broadcasted_iota(jnp.int32, (SUB, LANES), 1)
    odd = lax.rem(lax.axis_index("tile"), 2)
    pad6 = jnp.zeros((SUB - BANDS, LANES), F32)
    for base, part in ((24 - 24 * odd, got_near), (24 * odd, got_far), (16 - 8 * odd, near), (8 + 8 * odd, far)):
        for r in range(8):
            ext[base + r] = jnp.concatenate([part[pl.ds(r * BANDS, BANDS), :], pad6], axis=0)
    tk[...] = jnp.zeros((SUB, LANES), F32)
    tk[0:BANDS, 0:TAPS] = taps[...]
    sv = jnp.zeros((SUB, LANES), jnp.int32)
    for b in range(BANDS):
        sv = jnp.where(row16 == b, sizes[b], sv)
    kern = jnp.where((jnp.abs(lane16 - RADIUS) <= sv) & (lane16 < TAPS) & (row16 < BANDS), tk[...], 0.0)
    norm = jnp.sum(kern, axis=1, keepdims=True)
    norm = jnp.where(row16 < BANDS, jnp.broadcast_to(norm, (SUB, LANES)), 1.0)
    kern = kern / (norm * norm)
    kv = [jnp.broadcast_to(kern[:, t : t + 1], (SUB, LANES)) for t in range(TAPS)]
    z = jnp.zeros((32, LANES), BF)
    for r in range(16):
        f = kv[0] * ext[r]
        for t in range(1, TAPS):
            f = f + kv[t] * ext[r + t]
        w = jnp.concatenate([wt[pl.ds(r, BANDS, stride=16), :], pad6], axis=0)
        wf = w * f
        ff_ref[pl.ds(r, 1), :] = jnp.sum(wf * f, axis=0, keepdims=True)
        at = pl.ds((r % 2) * LANES, LANES)
        for ref, x in ((fc_ref, wf * SCALE), (ft_ref, w)):
            a, b, c = split3(x)
            ref[r // 2, :, at] = jnp.concatenate([a, b, a, c, b, a, z], axis=0)


def rows(got_far, got_near, far, near, wt, taps, sizes):
    vm = pl.BlockSpec(memory_space=pltpu.VMEM)
    sm = pl.BlockSpec(memory_space=pltpu.SMEM)
    on_chip = lambda x: pltpu.with_memory_space_constraint(x, pltpu.VMEM)
    side = pltpu.VMEM((8, LANES, 2 * LANES), BF)
    return pl.pallas_call(
        rows_kernel,
        out_shape=(side, side, pltpu.VMEM((16, LANES), F32)),
        in_specs=[vm, vm, vm, vm, vm, vm, sm],
        out_specs=(vm, vm, vm),
        scratch_shapes=[pltpu.VMEM((32, SUB, LANES), F32), pltpu.VMEM((SUB, LANES), F32)],
        name="rows",
    )(on_chip(got_far), on_chip(got_near), on_chip(far), on_chip(near), on_chip(wt.reshape(BANDS * 16, LANES)), taps, sizes)


def fit_kernel(fc_ref, ft_ref, ff_ref, bank, pm_ref, le_ref, lc, lt, cs, g_ref, e_ref, *, KC):
    row16 = lax.broadcasted_iota(jnp.int32, (SUB, LANES), 0)

    def lhs_prep(s):
        zeros32 = jnp.zeros((32, LANES), F32)
        blk = bank[s]
        T = jnp.where(row16 < BANDS, blk, 0.0)
        for dst, X in ((lc, T), (lt, T * T)):
            a, b, c = (v.astype(F32) for v in split3(X))
            st = jnp.concatenate([a, a, b, a, b, c, zeros32], axis=0)
            dst[pl.ds(s * LANES, LANES), :] = st.T.astype(BF)
        cc = (2.0 * blk + 1.0) * (1.0 / 128.0)
        cc = jnp.where(row16 == 13, 1.0, jnp.where((row16 >= 10) & (row16 < 13), cc, 0.0))
        cs[:, pl.ds(s * LANES, LANES)] = cc.astype(BF)

    NT = lc.shape[0]
    n1 = NT // KC

    def phase1(ch, Fc, Ft, m):
        c = jnp.dot(lc[pl.ds(ch * KC, KC), :], Fc, preferred_element_type=F32)
        t = jnp.dot(lt[pl.ds(ch * KC, KC), :], Ft, preferred_element_type=F32)
        g = c * c / t
        g_ref[pl.ds(ch * KC, KC), :] = g
        mm = jnp.max(g.reshape(KC // 8, 8, 256), axis=0)
        return mm if m is None else jnp.maximum(m, mm)

    def exps(k, m):
        e_ref[pl.ds(k * KC, KC), :] = jnp.exp2(g_ref[pl.ds(k * KC, KC), :] - m).astype(BF)

    def edot(k, acc):
        d = jnp.dot(cs[:, pl.ds(k * KC, KC)], e_ref[pl.ds(k * KC, KC), :], preferred_element_type=F32)
        return d if acc is None else acc + d

    def finish(r2, m, acc):
        tot = acc[13:14]
        pm = acc[10:13] / tot
        le = m * LN2 + jnp.log(tot)
        for j in range(2):
            sl = slice(j * LANES, j * LANES + LANES)
            for q in range(3):
                pm_ref[q, pl.ds(2 * r2 + j, 1), :] = pm[q : q + 1, sl]
            at = pl.ds(2 * r2 + j, 1)
            le_ref[at, :] = le[:, sl] - 0.5 * ff_ref[at, :]

    Fc, Ft = fc_ref[0], ft_ref[0]
    m = None
    for ch in range(n1):
        for s in range(ch * KC // LANES, (ch + 1) * KC // LANES):
            lhs_prep(s)
        m = phase1(ch, Fc, Ft, m)
    m0 = jnp.max(m, axis=0, keepdims=True)

    def body(i, mp):
        Fc, Ft = fc_ref[i], ft_ref[i]
        m = acc = None
        for ch in range(n1):
            if ch >= 1:
                acc = edot(ch - 1, acc)
            exps(ch, mp)
            m = phase1(ch, Fc, Ft, m)
        acc = edot(n1 - 1, acc)
        finish(i - 1, mp, acc)
        return jnp.max(m, axis=0, keepdims=True)

    mp = lax.fori_loop(1, 8, body, m0)
    acc = None
    for k in range(n1):
        exps(k, mp)
        acc = edot(k, acc)
    finish(7, mp, acc)


def fit(fc, ft, ff, bank, KC=256):
    vm = pl.BlockSpec(memory_space=pltpu.VMEM)
    nt = bank.shape[0] * LANES
    on_chip = lambda x: pltpu.with_memory_space_constraint(x, pltpu.VMEM)
    return pl.pallas_call(
        functools.partial(fit_kernel, KC=KC),
        out_shape=(jax.ShapeDtypeStruct((3, 16, LANES), F32), jax.ShapeDtypeStruct((16, LANES), F32)),
        in_specs=[vm] * 4,
        out_specs=(vm, vm),
        scratch_shapes=[
            pltpu.VMEM((nt, LANES), BF),
            pltpu.VMEM((nt, LANES), BF),
            pltpu.VMEM((SUB, nt), BF),
            pltpu.VMEM((nt, 256), F32),
            pltpu.VMEM((nt, 256), BF),
        ],
        name="fit",
    )(on_chip(fc), on_chip(ft), on_chip(ff), on_chip(bank))


def swaps(start, count):
    pairs = [(i, i + 1) for i in range(start, count - 1, 2)]
    return pairs + [(j, i) for i, j in pairs]


def body(sky_image, inverse_var, kernel_taps, kernel_sizes, templates, grid_index):
    shards = lax.axis_size("tmpl")
    tiles = lax.axis_size("tile")
    bank = bank_copies(templates, grid_index, shards)
    bank = lax.all_to_all(bank, "tmpl", split_axis=0, concat_axis=0, tiled=True)
    far, near, weight = prep(sky_image, inverse_var, kernel_taps, kernel_sizes, shards)
    got_far = lax.ppermute(far, "tile", swaps(1, tiles))
    got_near = lax.ppermute(near, "tile", swaps(0, tiles))
    fc, ft, ff = rows(got_far, got_near, far, near, weight, kernel_taps, kernel_sizes)
    return fit(fc, ft, ff, bank)


def solution(mesh):
    placed = (
        P(None, "tile", None),
        P(None, "tile", None),
        P(),
        P(),
        P(None, "tmpl"),
        P(None, "tmpl"),
    )
    return jax.shard_map(
        body,
        mesh=mesh,
        in_specs=placed,
        out_specs=(P(None, "tile", "tmpl"), P("tile", "tmpl")),
        check_vma=False,
    )
```

time: 30.8 us -> 29 us (0.942)
  waiting for transfers between devices: 4.6 us -> 1.18 us
  Pallas kernels: 10.5 us -> 12 us
    ppermute x2, waiting for transfers between devices: 4.6 us -> 1.18 us  [the longest x1 1.17 us: body(): got_near = lax.ppermute(near, 'tile', swaps(0, tiles))]
    pallas_call x1 -> x3, Pallas kernels: 2.13 us -> 4.21 us  [the longest x1 1.51 us: bank_copies(): pl.pallas_call(bank_kernel, out_shape=jax.ShapeDtypeStruct((shards, SUB,...]
    pallas_call x1, Pallas kernels: 8.4 us -> 7.83 us  [fit(): pl.pallas_call(functools.partial(fit_kernel, KC=KC), out_shape=(jax.Shape...]
  transfers between devices with their start and end apart: 3 -> 3, of which waited for: 1 -> 1; matrix products, arithmetic and copies ran while one was open for 0% -> 0% of each run, Pallas kernels for 0% -> 9%
where the time goes in v3:
time: 29 us; the launch traced here: 28.6 us
  starting transfers between devices  14.7 us (51%)
  Pallas kernels  12 us (41%)
  waiting for transfers between devices  1.18 us (4%)
  between operations  0.68 us (2%)
    pallas_call x1, Pallas kernels, fit(): pl.pallas_call(functools.partial(fit_kernel, KC=KC), out_shape=(jax.Shape...  7.83 us
    all_to_all x1, starting transfers between devices, body(): bank = lax.all_to_all(bank, 'tmpl', split_axis=0, concat_axis=0, tiled=True)  6.93 us
    ppermute x1, starting transfers between devices, body(): got_far = lax.ppermute(far, 'tile', swaps(1, tiles))  5.88 us
    ppermute x1, starting transfers between devices, body(): got_near = lax.ppermute(near, 'tile', swaps(0, tiles))  1.92 us
    pallas_call x1, Pallas kernels, bank_copies(): pl.pallas_call(bank_kernel, out_shape=jax.ShapeDtypeStruct((shards, SUB,...  1.51 us
    pallas_call x1, Pallas kernels, prep(): pl.pallas_call(functools.partial(prep_kernel, shards=shards), out_shape=(...  1.45 us
    pallas_call x1, Pallas kernels, rows(): pl.pallas_call(rows_kernel, out_shape=(side, side, pltpu.VMEM((16, LANES)...  1.24 us
    ppermute x1, waiting for transfers between devices, body(): got_near = lax.ppermute(near, 'tile', swaps(0, tiles))  1.17 us
  transfers between devices with their start and end apart: 3, of which 1 were waited for; matrix products, arithmetic and copies ran while one was open for 0% of the time, Pallas kernels for 9%

profile of v3, /device:TPU:227, one launch (start us, length us, event | category | flops | bytes accessed | tf_op | source)
XLA Modules:
  0.0 28.6 jit_solution(16346157456345718151)
XLA Ops:
  0.6 1.5 %bank.1 = f32[16,16,128]{2,1,0:T(8,128)} custom-call(f32[10,128]{1,0:T(8,128)} %templates.1, s32[3,128]{1,0:T(4,128)} %grid_index.1), custom_call_target="tpu_custom_call" | custom-call | tf_op jit(solution)/shard_map/bank/pallas_call | solution.py:43
  2.2 6.9 %all-to-all-start = ((f32[16,16,128]{2,1,0:T(8,128)}), f32[16,16,128]{2,1,0:T(8,128)S(1)}, u32[]{:S(2)}, u32[]{:S(2)}) async-start(f32[16,16,128]{2,1,0:T(8,128)} %bank.1), calls=%async_computation | async-start | bytes 262144 | tf_op jit(solution)/shard_map/all_to_all | solution.py:266
  9.1 1.4 %prep.1 = (f32[80,128]{1,0:T(8,128)S(1)}, f32[80,128]{1,0:T(8,128)S(1)}, f32[10,16,128]{2,1,0:T(8,128)S(1)}) custom-call(f32[10,16,2048]{2,1,0:T(8,128)} %sky.1, f32[10,16,2048]{2,1,0:T(8,128)} %ivar.1, f32[10,17]{1,0:T(8,128)} %taps.3, s32[10]{0:T(128)} %sizes.3), custom_call_target="tpu_custom_call" | custom-call | tf_op jit(solution)/shard_map/prep/pallas_call | solution.py:95
  10.5 5.9 %collective-permute-start = (f32[80,128]{1,0:T(8,128)S(1)}, f32[80,128]{1,0:T(8,128)S(1)}, u32[]{:S(2)}, u32[]{:S(2)}) collective-permute-start(f32[80,128]{1,0:T(8,128)S(1)} %get-tuple-element.8.far), channel_id=1, source_target_pairs={{16,32},{48,64},{80,96},{112,128},{144,160},{176,192},{208,224},{2... | collective-permute-start | bytes 122888 | tf_op jit(solution)/shard_map/ppermute | solution.py:268
  16.4 1.9 %collective-permute-start.1 = (f32[80,128]{1,0:T(8,128)S(1)}, f32[80,128]{1,0:T(8,128)S(1)}, u32[]{:S(2)}, u32[]{:S(2)}) collective-permute-start(f32[80,128]{1,0:T(8,128)S(1)} %get-tuple-element.9.near), channel_id=1, source_target_pairs={{0,16},{32,48},{64,80},{96,112},{128,144},{160,176},{192,208},{224... | collective-permute-start | bytes 122888 | tf_op jit(solution)/shard_map/ppermute | solution.py:269
  18.4 0.0 collective-permute-done.got_far
  18.4 1.2 %collective-permute-done.1.got_near = f32[80,128]{1,0:T(8,128)S(1)} collective-permute-done((f32[80,128]{1,0:T(8,128)S(1)}, f32[80,128]{1,0:T(8,128)S(1)}, u32[]{:S(2)}, u32[]{:S(2)}) %collective-permute-start.1) | collective-permute-done | bytes 40992 | tf_op jit(solution)/shard_map/ppermute | solution.py:269
  19.5 1.2 %rows.1 = (bf16[8,128,256]{2,1,0:T(8,128)(2,1)S(1)}, bf16[8,128,256]{2,1,0:T(8,128)(2,1)S(1)}, f32[16,128]{1,0:T(8,128)S(1)}) custom-call(f32[80,128]{1,0:T(8,128)S(1)} %collective-permute-done.got_far, f32[80,128]{1,0:T(8,128)S(1)} %collective-permute-done.1.got_near, f32[80,128]{1,0:T(8,128)S(1)} %get-tuple-element.8.far, ...), custom_call_target="tpu_custom_call" | custom-call | tf_op jit(solution)/shard_map/rows/pallas_call | solution.py:155
  20.8 0.0 all-to-all-done.bank
  20.8 7.8 %fit.1 = (f32[3,16,128]{2,1,0:T(8,128)}, f32[16,128]{1,0:T(8,128)}) custom-call(bf16[8,128,256]{2,1,0:T(8,128)(2,1)S(1)} %get-tuple-element.11.fc_ref, bf16[8,128,256]{2,1,0:T(8,128)(2,1)S(1)} %get-tuple-element.12.ft_ref, f32[16,128]{1,0:T(8,128)S(1)} %get-tuple-element.13.ff_ref, f32[16,16,128]{2,1,0:T(8,128)S(1)} %all-to-all-done.bank), custom_call_target="tpu_custom_call" | custom-call | tf_op jit(solution)/shard_map/fit/pallas_call | solution.py:241
Async XLA Ops:
  2.2 18.6 %all-to-all-start = ((f32[16,16,128]{2,1,0:T(8,128)}), f32[16,16,128]{2,1,0:T(8,128)S(1)}, u32[]{:S(2)}, u32[]{:S(2)}) async-start(f32[16,16,128]{2,1,0:T(8,128)} %bank.1), calls=%async_computation | async-start | bytes 262144 | tf_op jit(solution)/shard_map/all_to_all | solution.py:266
  10.5 7.8 %collective-permute-start = (f32[80,128]{1,0:T(8,128)S(1)}, f32[80,128]{1,0:T(8,128)S(1)}, u32[]{:S(2)}, u32[]{:S(2)}) collective-permute-start(f32[80,128]{1,0:T(8,128)S(1)} %get-tuple-element.8.far), channel_id=1, source_target_pairs={{16,32},{48,64},{80,96},{112,128},{144,160},{176,192},{208,224},{2... | collective-permute-start | bytes 122888 | tf_op jit(solution)/shard_map/ppermute | solution.py:268
  16.4 3.1 %collective-permute-start.1 = (f32[80,128]{1,0:T(8,128)S(1)}, f32[80,128]{1,0:T(8,128)S(1)}, u32[]{:S(2)}, u32[]{:S(2)}) collective-permute-start(f32[80,128]{1,0:T(8,128)S(1)} %get-tuple-element.9.near), channel_id=1, source_target_pairs={{0,16},{32,48},{64,80},{96,112},{128,144},{160,176},{192,208},{224... | collective-permute-start | bytes 122888 | tf_op jit(solution)/shard_map/ppermute | solution.py:269

commit v4 on v3

v4 whole, which is shorter than its diff:
```python
import functools
import math

import jax
import jax.numpy as jnp
from jax import lax
from jax.experimental import pallas as pl
from jax.experimental.pallas import tpu as pltpu
from jax.sharding import PartitionSpec as P

BANDS = 10
RADIUS = 8
TAPS = 2 * RADIUS + 1
LANES = 128
SUB = 16
SCALE = math.sqrt(0.5 / math.log(2.0))
LN2 = math.log(2.0)
BF = jnp.bfloat16
F32 = jnp.float32


def head_kernel(
    sky, ivar, taps, sizes, templates, grid_index, bank, cols, weight, kv, rows, gi, tk, sz, sems, bank_sems
):
    c = lax.axis_index("tmpl")
    shards = bank.shape[0]
    at = lambda i: pl.ds(pl.multiple_of(i * LANES, LANES), LANES)
    reads = [
        pltpu.make_async_copy(templates, rows.at[0:BANDS], sems.at[0]),
        pltpu.make_async_copy(grid_index, gi, sems.at[1]),
        pltpu.make_async_copy(taps, tk, sems.at[2]),
        pltpu.make_async_copy(sizes, sz, sems.at[3]),
        pltpu.make_async_copy(sky.at[:, :, at(jnp.maximum(c - 1, 0))], cols.at[0], sems.at[4]),
        pltpu.make_async_copy(sky.at[:, :, at(c)], cols.at[1], sems.at[5]),
        pltpu.make_async_copy(sky.at[:, :, at(jnp.minimum(c + 1, shards - 1))], cols.at[2], sems.at[6]),
        pltpu.make_async_copy(ivar.at[:, :, at(c)], weight, sems.at[7]),
    ]
    for copy in reads:
        copy.start()
    rows[BANDS + 3 : SUB] = jnp.zeros((SUB - BANDS - 3, LANES), F32)
    reads[1].wait()
    rows[BANDS : BANDS + 3] = gi[...].astype(F32)
    reads[0].wait()
    writes = [pltpu.make_async_copy(rows, bank.at[s], bank_sems.at[s]) for s in range(shards)]
    for copy in writes:
        copy.start()
    reads[2].wait()
    reads[3].wait()
    band = lax.broadcasted_iota(jnp.int32, (BANDS, TAPS), 0)
    tap = lax.broadcasted_iota(jnp.int32, (BANDS, TAPS), 1)
    half = jnp.zeros((BANDS, TAPS), jnp.int32)
    for b in range(BANDS):
        half = jnp.where(band == b, sz[b], half)
    kern = jnp.where(jnp.abs(tap - RADIUS) <= half, tk[...], 0.0)
    kern = kern / jnp.sum(kern, axis=1, keepdims=True)
    for t in range(TAPS):
        kv[t, 0:BANDS] = jnp.broadcast_to(kern[:, t : t + 1], (BANDS, LANES))
        kv[t, BANDS:SUB] = jnp.zeros((SUB - BANDS, LANES), F32)
    for copy in reads[4:]:
        copy.wait()
    for copy in writes:
        copy.wait()


def head(sky, ivar, taps, sizes, templates, grid_index, shards):
    hbm = pl.BlockSpec(memory_space=pl.ANY)
    vm = pl.BlockSpec(memory_space=pltpu.VMEM)
    return pl.pallas_call(
        head_kernel,
        out_shape=(
            jax.ShapeDtypeStruct((shards, SUB, LANES), F32),
            pltpu.VMEM((3, BANDS, 16, LANES), F32),
            pltpu.VMEM((BANDS, 16, LANES), F32),
            pltpu.VMEM((TAPS, SUB, LANES), F32),
        ),
        in_specs=[hbm] * 6,
        out_specs=(hbm, vm, vm, vm),
        scratch_shapes=[
            pltpu.VMEM((SUB, LANES), F32),
            pltpu.VMEM((3, LANES), jnp.int32),
            pltpu.VMEM((BANDS, TAPS), F32),
            pltpu.SMEM((BANDS,), jnp.int32),
            pltpu.SemaphoreType.DMA((8,)),
            pltpu.SemaphoreType.DMA((shards,)),
        ],
        name="head",
    )(sky, ivar, taps, sizes, templates, grid_index)


def columns_kernel(cols, kv, far, near, *, shards):
    c = lax.axis_index("tmpl")
    odd = lax.rem(lax.axis_index("tile"), 2) == 1
    lane = lax.broadcasted_iota(jnp.int32, (16, LANES), 1)
    right_ok = jnp.where(c < shards - 1, 1.0, 0.0)
    left_ok = jnp.where(c > 0, 1.0, 0.0)
    for b in range(BANDS):
        main = cols[1, b]
        side = jnp.where(lane < LANES // 2, cols[2, b] * right_ok, cols[0, b] * left_ok)
        tap = lambda t: jnp.broadcast_to(kv[t, b : b + 1, :], (16, LANES))
        acc = main * tap(RADIUS)
        for d in range(1, RADIUS + 1):
            up = pltpu.roll(jnp.where(lane >= d, main, side), LANES - d, 1)
            down = pltpu.roll(jnp.where(lane < LANES - d, main, side), d, 1)
            acc = acc + up * tap(RADIUS + d)
            acc = acc + down * tap(RADIUS - d)
        far[pl.ds(b, 8, stride=BANDS), :] = jnp.where(odd, acc[8:], acc[:8])
        near[pl.ds(b, 8, stride=BANDS), :] = jnp.where(odd, acc[:8], acc[8:])


def on_chip(x):
    return pltpu.with_memory_space_constraint(x, pltpu.VMEM)


def columns(cols, kv, shards):
    vm = pl.BlockSpec(memory_space=pltpu.VMEM)
    part = pltpu.VMEM((8 * BANDS, LANES), F32)
    return pl.pallas_call(
        functools.partial(columns_kernel, shards=shards),
        out_shape=(part, part),
        in_specs=[vm] * 2,
        out_specs=(vm,) * 2,
        name="columns",
    )(on_chip(cols), on_chip(kv))


def split3(x):
    a = x.astype(BF)
    r = x - a.astype(F32)
    b = r.astype(BF)
    r = r - b.astype(F32)
    return a, b, r.astype(BF)


def rows_kernel(got_far, got_near, far, near, wt, kv, fc_ref, ft_ref, ff_ref, ext):
    odd = lax.rem(lax.axis_index("tile"), 2)
    pad6 = jnp.zeros((SUB - BANDS, LANES), F32)
    for base, part in ((24 - 24 * odd, got_near), (24 * odd, got_far), (16 - 8 * odd, near), (8 + 8 * odd, far)):
        for r in range(8):
            ext[base + r] = jnp.concatenate([part[pl.ds(r * BANDS, BANDS), :], pad6], axis=0)
    z = jnp.zeros((32, LANES), BF)
    for r in range(16):
        f = kv[0] * ext[r]
        for t in range(1, TAPS):
            f = f + kv[t] * ext[r + t]
        w = jnp.concatenate([wt[pl.ds(r, BANDS, stride=16), :], pad6], axis=0)
        wf = w * f
        ff_ref[pl.ds(r, 1), :] = jnp.sum(wf * f, axis=0, keepdims=True)
        at = pl.ds((r % 2) * LANES, LANES)
        for ref, x in ((fc_ref, wf * SCALE), (ft_ref, w)):
            a, b, c = split3(x)
            ref[r // 2, :, at] = jnp.concatenate([a, b, a, c, b, a, z], axis=0)


def rows(got_far, got_near, far, near, wt, kv):
    vm = pl.BlockSpec(memory_space=pltpu.VMEM)
    side = pltpu.VMEM((8, LANES, 2 * LANES), BF)
    return pl.pallas_call(
        rows_kernel,
        out_shape=(side, side, pltpu.VMEM((16, LANES), F32)),
        in_specs=[vm] * 6,
        out_specs=(vm,) * 3,
        scratch_shapes=[pltpu.VMEM((32, SUB, LANES), F32)],
        name="rows",
    )(on_chip(got_far), on_chip(got_near), on_chip(far), on_chip(near), on_chip(wt.reshape(BANDS * 16, LANES)), on_chip(kv))


def fit_kernel(fc_ref, ft_ref, ff_ref, bank, pm_ref, le_ref, lc, lt, cs, g_ref, e_ref, *, KC):
    row16 = lax.broadcasted_iota(jnp.int32, (SUB, LANES), 0)

    def lhs_prep(s):
        zeros32 = jnp.zeros((32, LANES), F32)
        blk = bank[s]
        T = jnp.where(row16 < BANDS, blk, 0.0)
        for dst, X in ((lc, T), (lt, T * T)):
            a, b, c = (v.astype(F32) for v in split3(X))
            st = jnp.concatenate([a, a, b, a, b, c, zeros32], axis=0)
            dst[pl.ds(s * LANES, LANES), :] = st.T.astype(BF)
        cc = (2.0 * blk + 1.0) * (1.0 / 128.0)
        cc = jnp.where(row16 == 13, 1.0, jnp.where((row16 >= 10) & (row16 < 13), cc, 0.0))
        cs[:, pl.ds(s * LANES, LANES)] = cc.astype(BF)

    NT = lc.shape[0]
    n1 = NT // KC

    def phase1(ch, Fc, Ft, m):
        c = jnp.dot(lc[pl.ds(ch * KC, KC), :], Fc, preferred_element_type=F32)
        t = jnp.dot(lt[pl.ds(ch * KC, KC), :], Ft, preferred_element_type=F32)
        g = c * c / t
        g_ref[pl.ds(ch * KC, KC), :] = g
        mm = jnp.max(g.reshape(KC // 8, 8, 256), axis=0)
        return mm if m is None else jnp.maximum(m, mm)

    def exps(k, m):
        e_ref[pl.ds(k * KC, KC), :] = jnp.exp2(g_ref[pl.ds(k * KC, KC), :] - m).astype(BF)

    def edot(k, acc):
        d = jnp.dot(cs[:, pl.ds(k * KC, KC)], e_ref[pl.ds(k * KC, KC), :], preferred_element_type=F32)
        return d if acc is None else acc + d

    def finish(r2, m, acc):
        tot = acc[13:14]
        pm = acc[10:13] / tot
        le = m * LN2 + jnp.log(tot)
        for j in range(2):
            sl = slice(j * LANES, j * LANES + LANES)
            for q in range(3):
                pm_ref[q, pl.ds(2 * r2 + j, 1), :] = pm[q : q + 1, sl]
            at = pl.ds(2 * r2 + j, 1)
            le_ref[at, :] = le[:, sl] - 0.5 * ff_ref[at, :]

    Fc, Ft = fc_ref[0], ft_ref[0]
    m = None
    for ch in range(n1):
        for s in range(ch * KC // LANES, (ch + 1) * KC // LANES):
            lhs_prep(s)
        m = phase1(ch, Fc, Ft, m)
    m0 = jnp.max(m, axis=0, keepdims=True)

    def body(i, mp):
        Fc, Ft = fc_ref[i], ft_ref[i]
        m = acc = None
        for ch in range(n1):
            exps(ch, mp)
            m = phase1(ch, Fc, Ft, m)
            if ch >= 1:
                acc = edot(ch - 1, acc)
        acc = edot(n1 - 1, acc)
        finish(i - 1, mp, acc)
        return jnp.max(m, axis=0, keepdims=True)

    mp = lax.fori_loop(1, 8, body, m0)
    acc = None
    for k in range(n1):
        exps(k, mp)
        acc = edot(k, acc)
    finish(7, mp, acc)


def fit(fc, ft, ff, bank, KC=256):
    vm = pl.BlockSpec(memory_space=pltpu.VMEM)
    nt = bank.shape[0] * LANES
    return pl.pallas_call(
        functools.partial(fit_kernel, KC=KC),
        out_shape=(jax.ShapeDtypeStruct((3, 16, LANES), F32), jax.ShapeDtypeStruct((16, LANES), F32)),
        in_specs=[vm] * 4,
        out_specs=(vm, vm),
        scratch_shapes=[
            pltpu.VMEM((nt, LANES), BF),
            pltpu.VMEM((nt, LANES), BF),
            pltpu.VMEM((SUB, nt), BF),
            pltpu.VMEM((nt, 256), F32),
            pltpu.VMEM((nt, 256), BF),
        ],
        name="fit",
    )(on_chip(fc), on_chip(ft), on_chip(ff), on_chip(bank))


def swaps(start, count):
    pairs = [(i, i + 1) for i in range(start, count - 1, 2)]
    return pairs + [(j, i) for i, j in pairs]


def body(sky_image, inverse_var, kernel_taps, kernel_sizes, templates, grid_index):
    shards = lax.axis_size("tmpl")
    tiles = lax.axis_size("tile")
    bank, cols, weight, kv = head(sky_image, inverse_var, kernel_taps, kernel_sizes, templates, grid_index, shards)
    bank = lax.all_to_all(bank, "tmpl", split_axis=0, concat_axis=0, tiled=True)
    far, near = columns(cols, kv, shards)
    got_far = lax.ppermute(far, "tile", swaps(1, tiles))
    got_near = lax.ppermute(near, "tile", swaps(0, tiles))
    fc, ft, ff = rows(got_far, got_near, far, near, weight, kv)
    return fit(fc, ft, ff, bank)


def solution(mesh):
    placed = (
        P(None, "tile", None),
        P(None, "tile", None),
        P(),
        P(),
        P(None, "tmpl"),
        P(None, "tmpl"),
    )
    return jax.shard_map(
        body,
        mesh=mesh,
        in_specs=placed,
        out_specs=(P(None, "tile", "tmpl"), P("tile", "tmpl")),
        check_vma=False,
    )
```

time: 29 us -> 26.6 us (0.917)
  Pallas kernels: 12 us -> 9.68 us
    pallas_call x2, Pallas kernels: 2.96 us -> 1.98 us  [the longest x1 1.57 us: head(): pl.pallas_call(head_kernel, out_shape=(jax.ShapeDtypeStruct((shards, SUB,...]
    pallas_call x1, Pallas kernels: 1.24 us -> 0.33 us  [rows(): pl.pallas_call(rows_kernel, out_shape=(side, side, pltpu.VMEM((16, LANES)...]
    pallas_call x1, Pallas kernels: 7.83 us -> 7.37 us  [fit(): pl.pallas_call(functools.partial(fit_kernel, KC=KC), out_shape=(jax.Shape...]
  transfers between devices with their start and end apart: 3 -> 3, of which waited for: 1 -> 1; matrix products, arithmetic and copies ran while one was open for 0% -> 0% of each run, Pallas kernels for 9% -> 3%
where the time goes in v4:
time: 26.6 us; the launch traced here: 26.3 us
  starting transfers between devices  14.7 us (55%)
  Pallas kernels  9.68 us (36%)
  waiting for transfers between devices  1.18 us (4%)
  between operations  0.68 us (3%)
    pallas_call x1, Pallas kernels, fit(): pl.pallas_call(functools.partial(fit_kernel, KC=KC), out_shape=(jax.Shape...  7.37 us
    all_to_all x1, starting transfers between devices, body(): bank = lax.all_to_all(bank, 'tmpl', split_axis=0, concat_axis=0, tiled=True)  6.93 us
    ppermute x1, starting transfers between devices, body(): got_far = lax.ppermute(far, 'tile', swaps(1, tiles))  5.88 us
    ppermute x1, starting transfers between devices, body(): got_near = lax.ppermute(near, 'tile', swaps(0, tiles))  1.92 us
    pallas_call x1, Pallas kernels, head(): pl.pallas_call(head_kernel, out_shape=(jax.ShapeDtypeStruct((shards, SUB,...  1.57 us
    ppermute x1, waiting for transfers between devices, body(): got_near = lax.ppermute(near, 'tile', swaps(0, tiles))  1.17 us
  transfers between devices with their start and end apart: 3, of which 1 were waited for; matrix products, arithmetic and copies ran while one was open for 0% of the time, Pallas kernels for 3%

profile of v4, /device:TPU:227, one launch (start us, length us, event | category | flops | bytes accessed | tf_op | source)
XLA Modules:
  0.0 26.3 jit_solution(1965500470692273495)
XLA Ops:
  0.6 1.6 %head.1 = (f32[16,16,128]{2,1,0:T(8,128)}, f32[3,10,16,128]{3,2,1,0:T(8,128)S(1)}, f32[10,16,128]{2,1,0:T(8,128)S(1)}, f32[17,16,128]{2,1,0:T(8,128)S(1)}) custom-call(f32[10,16,2048]{2,1,0:T(8,128)} %sky.1, f32[10,16,2048]{2,1,0:T(8,128)} %ivar.1, f32[10,17]{1,0:T(8,128)} %taps.1, s32[10]{0:T(128)} %sizes.1, f32[10,128]{1,0:T(8,128)} %templates.1, ...), custom_call_target="tpu_custom_call" | custom-call | tf_op jit(solution)/shard_map/head/pallas_call | solution.py:68
  2.2 6.9 %all-to-all-start = ((f32[16,16,128]{2,1,0:T(8,128)}), f32[16,16,128]{2,1,0:T(8,128)S(1)}, u32[]{:S(2)}, u32[]{:S(2)}) async-start(f32[16,16,128]{2,1,0:T(8,128)} %get-tuple-element.19), calls=%async_computation | async-start | bytes 262144 | tf_op jit(solution)/shard_map/all_to_all | solution.py:267
  9.1 0.4 %columns.1 = (f32[80,128]{1,0:T(8,128)S(1)}, f32[80,128]{1,0:T(8,128)S(1)}) custom-call(f32[3,10,16,128]{3,2,1,0:T(8,128)S(1)} %get-tuple-element.11.cols, f32[17,16,128]{2,1,0:T(8,128)S(1)} %get-tuple-element.12.kv), custom_call_target="tpu_custom_call" | custom-call | tf_op jit(solution)/shard_map/columns/pallas_call | solution.py:117
  9.6 5.9 %collective-permute-start = (f32[80,128]{1,0:T(8,128)S(1)}, f32[80,128]{1,0:T(8,128)S(1)}, u32[]{:S(2)}, u32[]{:S(2)}) collective-permute-start(f32[80,128]{1,0:T(8,128)S(1)} %get-tuple-element.13.far), channel_id=1, source_target_pairs={{16,32},{48,64},{80,96},{112,128},{144,160},{176,192},{208,224},{2... | collective-permute-start | bytes 122888 | tf_op jit(solution)/shard_map/ppermute | solution.py:269
  15.4 1.9 %collective-permute-start.1 = (f32[80,128]{1,0:T(8,128)S(1)}, f32[80,128]{1,0:T(8,128)S(1)}, u32[]{:S(2)}, u32[]{:S(2)}) collective-permute-start(f32[80,128]{1,0:T(8,128)S(1)} %get-tuple-element.14.near), channel_id=1, source_target_pairs={{0,16},{32,48},{64,80},{96,112},{128,144},{160,176},{192,208},{224... | collective-permute-start | bytes 122888 | tf_op jit(solution)/shard_map/ppermute | solution.py:270
  17.4 0.0 collective-permute-done.got_far
  17.4 1.2 %collective-permute-done.1.got_near = f32[80,128]{1,0:T(8,128)S(1)} collective-permute-done((f32[80,128]{1,0:T(8,128)S(1)}, f32[80,128]{1,0:T(8,128)S(1)}, u32[]{:S(2)}, u32[]{:S(2)}) %collective-permute-start.1) | collective-permute-done | bytes 40992 | tf_op jit(solution)/shard_map/ppermute | solution.py:270
  18.6 0.3 %rows.1 = (bf16[8,128,256]{2,1,0:T(8,128)(2,1)S(1)}, bf16[8,128,256]{2,1,0:T(8,128)(2,1)S(1)}, f32[16,128]{1,0:T(8,128)S(1)}) custom-call(f32[80,128]{1,0:T(8,128)S(1)} %collective-permute-done.got_far, f32[80,128]{1,0:T(8,128)S(1)} %collective-permute-done.1.got_near, f32[80,128]{1,0:T(8,128)S(1)} %get-tuple-element.13.far, ...), custom_call_target="tpu_custom_call" | custom-call | tf_op jit(solution)/shard_map/rows/pallas_call | solution.py:157
  18.9 0.0 all-to-all-done.bank
  18.9 7.4 %fit.1 = (f32[3,16,128]{2,1,0:T(8,128)}, f32[16,128]{1,0:T(8,128)}) custom-call(bf16[8,128,256]{2,1,0:T(8,128)(2,1)S(1)} %get-tuple-element.16.fc_ref, bf16[8,128,256]{2,1,0:T(8,128)(2,1)S(1)} %get-tuple-element.17.ft_ref, f32[16,128]{1,0:T(8,128)S(1)} %get-tuple-element.18.ff_ref, f32[16,16,128]{2,1,0:T(8,128)S(1)} %all-to-all-done.bank), custom_call_target="tpu_custom_call" | custom-call | tf_op jit(solution)/shard_map/fit/pallas_call | solution.py:242
Async XLA Ops:
  2.2 16.7 %all-to-all-start = ((f32[16,16,128]{2,1,0:T(8,128)}), f32[16,16,128]{2,1,0:T(8,128)S(1)}, u32[]{:S(2)}, u32[]{:S(2)}) async-start(f32[16,16,128]{2,1,0:T(8,128)} %get-tuple-element.19), calls=%async_computation | async-start | bytes 262144 | tf_op jit(solution)/shard_map/all_to_all | solution.py:267
  9.6 7.8 %collective-permute-start = (f32[80,128]{1,0:T(8,128)S(1)}, f32[80,128]{1,0:T(8,128)S(1)}, u32[]{:S(2)}, u32[]{:S(2)}) collective-permute-start(f32[80,128]{1,0:T(8,128)S(1)} %get-tuple-element.13.far), channel_id=1, source_target_pairs={{16,32},{48,64},{80,96},{112,128},{144,160},{176,192},{208,224},{2... | collective-permute-start | bytes 122888 | tf_op jit(solution)/shard_map/ppermute | solution.py:269
  15.4 3.1 %collective-permute-start.1 = (f32[80,128]{1,0:T(8,128)S(1)}, f32[80,128]{1,0:T(8,128)S(1)}, u32[]{:S(2)}, u32[]{:S(2)}) collective-permute-start(f32[80,128]{1,0:T(8,128)S(1)} %get-tuple-element.14.near), channel_id=1, source_target_pairs={{0,16},{32,48},{64,80},{96,112},{128,144},{160,176},{192,208},{224... | collective-permute-start | bytes 122888 | tf_op jit(solution)/shard_map/ppermute | solution.py:270

commit v5 on v4

--- a/solution.py
+++ b/solution.py
@@ -164,8 +164,31 @@
     )(on_chip(got_far), on_chip(got_near), on_chip(far), on_chip(near), on_chip(wt.reshape(BANDS * 16, LANES)), on_chip(kv))
 
 
-def fit_kernel(fc_ref, ft_ref, ff_ref, bank, pm_ref, le_ref, lc, lt, cs, g_ref, e_ref, *, KC):
+def fit_kernel(fc_ref, ft_ref, ff_ref, bank, pm_ref, le_ref, lc, lt, cs, g_ref, e_ref, *, R, L, NS, S, PR):
+    refs = (fc_ref, ft_ref, ff_ref, bank, pm_ref, le_ref, lc, lt, cs, g_ref, e_ref)
+    pl.run_scoped(
+        functools.partial(fit_body, *refs, R=R, L=L, S=S, PR=PR),
+        pltpu.ACC(0)((SUB, 256), F32),
+        pltpu.ACC(1)((SUB, 256), F32),
+        *[pltpu.ACC(0)((R, 256), F32) for _ in range(NS)],
+        *[pltpu.ACC(1)((R, 256), F32) for _ in range(NS)],
+    )
+
+
+def fit_body(
+    fc_ref, ft_ref, ff_ref, bank, pm_ref, le_ref, lc, lt, cs, g_ref, e_ref, acc_e0, acc_e1, *accs, R, L, S, PR
+):
+    NS = len(accs) // 2
+    acc_c, acc_t = accs[:NS], accs[NS:]
     row16 = lax.broadcasted_iota(jnp.int32, (SUB, LANES), 0)
+    NT = lc.shape[0]
+    KC = 256
+    n1 = NT // KC
+    G = KC // R
+    NG = NT // R
+    zl = jnp.zeros((R, LANES), BF)
+    zs = jnp.zeros((SUB, LANES), BF)
+    ze = jnp.zeros((LANES, 2 * LANES), BF)
 
     def lhs_prep(s):
         zeros32 = jnp.zeros((32, LANES), F32)
@@ -179,68 +202,113 @@
         cc = jnp.where(row16 == 13, 1.0, jnp.where((row16 >= 10) & (row16 < 13), cc, 0.0))
         cs[:, pl.ds(s * LANES, LANES)] = cc.astype(BF)
 
-    NT = lc.shape[0]
-    n1 = NT // KC
-
-    def phase1(ch, Fc, Ft, m):
-        c = jnp.dot(lc[pl.ds(ch * KC, KC), :], Fc, preferred_element_type=F32)
-        t = jnp.dot(lt[pl.ds(ch * KC, KC), :], Ft, preferred_element_type=F32)
+    def push(i, tile, stage):
+        for mxu, side in enumerate((fc_ref, ft_ref)):
+            e = ze if tile is None else e_ref[pl.ds(tile * KC + mxu * LANES, LANES), :]
+            pltpu.matmul_push_rhs(jnp.concatenate([side[i], e], axis=0), stage, mxu)
+
+    def issue(q, stage):
+        for acc, src in ((acc_c, lc), (acc_t, lt)):
+            pltpu.matmul_acc_lhs(acc[q % NS], jnp.concatenate([src[pl.ds(q * R, R), :], zl], axis=1), load_staged_rhs=stage)
+
+    def edot(tile, stage=None):
+        for mxu, acc in enumerate((acc_e0, acc_e1)):
+            lhs = jnp.concatenate([zs, cs[:, pl.ds(tile * KC + mxu * LANES, LANES)]], axis=1)
+            pltpu.matmul_acc_lhs(acc, lhs, load_staged_rhs=stage)
+
+    def take(q, m):
+        c = pltpu.matmul_pop(acc_c[q % NS])
+        t = pltpu.matmul_pop(acc_t[q % NS])
         g = c * c / t
-        g_ref[pl.ds(ch * KC, KC), :] = g
-        mm = jnp.max(g.reshape(KC // 8, 8, 256), axis=0)
+        g_ref[pl.ds(q * R, R), :] = g
+        mm = jnp.max(g.reshape(R // 8, 8, 256), axis=0)
         return mm if m is None else jnp.maximum(m, mm)
 
-    def exps(k, m):
-        e_ref[pl.ds(k * KC, KC), :] = jnp.exp2(g_ref[pl.ds(k * KC, KC), :] - m).astype(BF)
-
-    def edot(k, acc):
-        d = jnp.dot(cs[:, pl.ds(k * KC, KC)], e_ref[pl.ds(k * KC, KC), :], preferred_element_type=F32)
-        return d if acc is None else acc + d
-
-    def finish(r2, m, acc):
+    def exps(q, m):
+        rows = pl.ds(q * R, R)
+        e_ref[rows, :] = jnp.exp2(g_ref[rows, :] - m).astype(BF)
+
+    def finish(r2, m):
+        acc = pltpu.matmul_pop(acc_e0) + pltpu.matmul_pop(acc_e1)
         tot = acc[13:14]
         pm = acc[10:13] / tot
         le = m * LN2 + jnp.log(tot)
         for j in range(2):
             sl = slice(j * LANES, j * LANES + LANES)
+            at = pl.ds(2 * r2 + j, 1)
             for q in range(3):
-                pm_ref[q, pl.ds(2 * r2 + j, 1), :] = pm[q : q + 1, sl]
-            at = pl.ds(2 * r2 + j, 1)
+                pm_ref[q, at, :] = pm[q : q + 1, sl]
             le_ref[at, :] = le[:, sl] - 0.5 * ff_ref[at, :]
 
-    Fc, Ft = fc_ref[0], ft_ref[0]
+    top = lambda m: jnp.max(m, axis=0, keepdims=True)
+    last = 7
+    g_ref[pl.ds((NG - L) * R, L * R), :] = jnp.zeros((L * R, 256), F32)
+    e_ref[pl.ds((n1 - S) * KC, S * KC), :] = jnp.ones((S * KC, 256), BF)
+
+    push(0, None, 0)
     m = None
-    for ch in range(n1):
-        for s in range(ch * KC // LANES, (ch + 1) * KC // LANES):
-            lhs_prep(s)
-        m = phase1(ch, Fc, Ft, m)
-    m0 = jnp.max(m, axis=0, keepdims=True)
-
-    def body(i, mp):
-        Fc, Ft = fc_ref[i], ft_ref[i]
-        m = acc = None
-        for ch in range(n1):
-            exps(ch, mp)
-            m = phase1(ch, Fc, Ft, m)
-            if ch >= 1:
-                acc = edot(ch - 1, acc)
-        acc = edot(n1 - 1, acc)
-        finish(i - 1, mp, acc)
-        return jnp.max(m, axis=0, keepdims=True)
-
-    mp = lax.fori_loop(1, 8, body, m0)
-    acc = None
+    for q in range(NG):
+        if q * R % LANES == 0:
+            lhs_prep(q * R // LANES)
+        issue(q, 0 if q == 0 else None)
+        if q >= L:
+            m = take(q - L, m)
+    push(1, n1 - S, 0)
+
+    def body(i, carry):
+        m_before, old = carry
+        new = m = None
+        for q in range(NG):
+            k, r = divmod(q, G)
+            issue(q, k % 2 if r == 0 else None)
+            if r == 0:
+                if k == S:
+                    finish(jnp.maximum(i - 2, 0), old)
+                edot((k - S) % n1)
+            if q < L:
+                exps(NG + q - L, old)
+            else:
+                exps(q - L, new)
+            if r == PR:
+                step = k + 1
+                if step < n1:
+                    push(i, (step - S) % n1, step % 2)
+                else:
+                    push(jnp.minimum(i + 1, last), n1 - S, 0)
+            if q < L:
+                m_before = take(NG + q - L, m_before)
+                if q == L - 1:
+                    new = top(m_before)
+            else:
+                m = take(q - L, m)
+        return m, new
+
+    m, old = lax.fori_loop(1, last + 1, body, (m, jnp.zeros((1, 256), F32)))
+    for q in range(max(L, S * G)):
+        k, r = divmod(q, G)
+        if r == 0 and k < S:
+            edot(n1 - S + k, k % 2)
+        if q < L:
+            exps(NG + q - L, old)
+        if r == PR and k + 1 < S:
+            push(last, n1 - S + k + 1, (k + 1) % 2)
+        if q < L:
+            m = take(NG + q - L, m)
+    finish(last - 1, old)
+    new = top(m)
     for k in range(n1):
-        exps(k, mp)
-        acc = edot(k, acc)
-    finish(7, mp, acc)
-
-
-def fit(fc, ft, ff, bank, KC=256):
+        for r in range(G):
+            exps(k * G + r, new)
+        push(last, k, (S + k) % 2)
+        edot(k, (S + k) % 2)
+    finish(last, new)
+
+
+def fit(fc, ft, ff, bank, R=64, NS=8, L=7, S=3, PR=3):
     vm = pl.BlockSpec(memory_space=pltpu.VMEM)
     nt = bank.shape[0] * LANES
     return pl.pallas_call(
-        functools.partial(fit_kernel, KC=KC),
+        functools.partial(fit_kernel, R=R, L=L, NS=NS, S=S, PR=PR),
         out_shape=(jax.ShapeDtypeStruct((3, 16, LANES), F32), jax.ShapeDtypeStruct((16, LANES), F32)),
         in_specs=[vm] * 4,
         out_specs=(vm, vm),

time: 26.6 us -> 25.9 us (0.974)
  the two profiles are of different devices: /device:TPU:227 before, /device:TPU:99 now
where the time goes in v5:
time: 25.9 us; the launch traced here: 25.6 us
  starting transfers between devices  14.7 us (57%)
  Pallas kernels  9 us (35%)
  waiting for transfers between devices  1.18 us (5%)
  between operations  0.68 us (3%)
    all_to_all x1, starting transfers between devices, body(): bank = lax.all_to_all(bank, 'tmpl', split_axis=0, concat_axis=0, tiled=True)  6.93 us
    pallas_call x1, Pallas kernels, fit(): pl.pallas_call(functools.partial(fit_kernel, R=R, L=L, NS=NS, S=S, PR=PR)...  6.69 us
    ppermute x1, starting transfers between devices, body(): got_far = lax.ppermute(far, 'tile', swaps(1, tiles))  5.88 us
    ppermute x1, starting transfers between devices, body(): got_near = lax.ppermute(near, 'tile', swaps(0, tiles))  1.92 us
    pallas_call x1, Pallas kernels, head(): pl.pallas_call(head_kernel, out_shape=(jax.ShapeDtypeStruct((shards, SUB,...  1.57 us
    ppermute x1, waiting for transfers between devices, body(): got_near = lax.ppermute(near, 'tile', swaps(0, tiles))  1.17 us
  transfers between devices with their start and end apart: 3, of which 1 were waited for; matrix products, arithmetic and copies ran while one was open for 0% of the time, Pallas kernels for 3%

profile of v5, /device:TPU:99, one launch (start us, length us, event | category | flops | bytes accessed | tf_op | source)
XLA Modules:
  0.0 25.6 jit_solution(6347879652668562142)
XLA Ops:
  0.6 1.6 %head.1 = (f32[16,16,128]{2,1,0:T(8,128)}, f32[3,10,16,128]{3,2,1,0:T(8,128)S(1)}, f32[10,16,128]{2,1,0:T(8,128)S(1)}, f32[17,16,128]{2,1,0:T(8,128)S(1)}) custom-call(f32[10,16,2048]{2,1,0:T(8,128)} %sky.1, f32[10,16,2048]{2,1,0:T(8,128)} %ivar.1, f32[10,17]{1,0:T(8,128)} %taps.1, s32[10]{0:T(128)} %sizes.1, f32[10,128]{1,0:T(8,128)} %templates.1, ...), custom_call_target="tpu_custom_call" | custom-call | tf_op jit(solution)/shard_map/head/pallas_call | solution.py:68
  2.2 6.9 %all-to-all-start = ((f32[16,16,128]{2,1,0:T(8,128)}), f32[16,16,128]{2,1,0:T(8,128)S(1)}, u32[]{:S(2)}, u32[]{:S(2)}) async-start(f32[16,16,128]{2,1,0:T(8,128)} %get-tuple-element.19), calls=%async_computation | async-start | bytes 262144 | tf_op jit(solution)/shard_map/all_to_all | solution.py:335
  9.1 0.4 %columns.1 = (f32[80,128]{1,0:T(8,128)S(1)}, f32[80,128]{1,0:T(8,128)S(1)}) custom-call(f32[3,10,16,128]{3,2,1,0:T(8,128)S(1)} %get-tuple-element.11.cols, f32[17,16,128]{2,1,0:T(8,128)S(1)} %get-tuple-element.12.kv), custom_call_target="tpu_custom_call" | custom-call | tf_op jit(solution)/shard_map/columns/pallas_call | solution.py:117
  9.6 5.9 %collective-permute-start = (f32[80,128]{1,0:T(8,128)S(1)}, f32[80,128]{1,0:T(8,128)S(1)}, u32[]{:S(2)}, u32[]{:S(2)}) collective-permute-start(f32[80,128]{1,0:T(8,128)S(1)} %get-tuple-element.13.far), channel_id=1, source_target_pairs={{16,32},{48,64},{80,96},{112,128},{144,160},{176,192},{208,224},{2... | collective-permute-start | bytes 122888 | tf_op jit(solution)/shard_map/ppermute | solution.py:337
  15.4 1.9 %collective-permute-start.1 = (f32[80,128]{1,0:T(8,128)S(1)}, f32[80,128]{1,0:T(8,128)S(1)}, u32[]{:S(2)}, u32[]{:S(2)}) collective-permute-start(f32[80,128]{1,0:T(8,128)S(1)} %get-tuple-element.14.near), channel_id=1, source_target_pairs={{0,16},{32,48},{64,80},{96,112},{128,144},{160,176},{192,208},{224... | collective-permute-start | bytes 122888 | tf_op jit(solution)/shard_map/ppermute | solution.py:338
  17.4 0.0 collective-permute-done.got_far
  17.4 1.2 %collective-permute-done.1.got_near = f32[80,128]{1,0:T(8,128)S(1)} collective-permute-done((f32[80,128]{1,0:T(8,128)S(1)}, f32[80,128]{1,0:T(8,128)S(1)}, u32[]{:S(2)}, u32[]{:S(2)}) %collective-permute-start.1) | collective-permute-done | bytes 40992 | tf_op jit(solution)/shard_map/ppermute | solution.py:338
  18.6 0.3 %rows.1 = (bf16[8,128,256]{2,1,0:T(8,128)(2,1)S(1)}, bf16[8,128,256]{2,1,0:T(8,128)(2,1)S(1)}, f32[16,128]{1,0:T(8,128)S(1)}) custom-call(f32[80,128]{1,0:T(8,128)S(1)} %collective-permute-done.got_far, f32[80,128]{1,0:T(8,128)S(1)} %collective-permute-done.1.got_near, f32[80,128]{1,0:T(8,128)S(1)} %get-tuple-element.13.far, ...), custom_call_target="tpu_custom_call" | custom-call | tf_op jit(solution)/shard_map/rows/pallas_call | solution.py:157
  18.9 0.0 all-to-all-done.bank
  18.9 6.7 %fit.1 = (f32[3,16,128]{2,1,0:T(8,128)}, f32[16,128]{1,0:T(8,128)}) custom-call(bf16[8,128,256]{2,1,0:T(8,128)(2,1)S(1)} %get-tuple-element.16.fc_ref, bf16[8,128,256]{2,1,0:T(8,128)(2,1)S(1)} %get-tuple-element.17.ft_ref, f32[16,128]{1,0:T(8,128)S(1)} %get-tuple-element.18.ff_ref, f32[16,16,128]{2,1,0:T(8,128)S(1)} %all-to-all-done.bank), custom_call_target="tpu_custom_call" | custom-call | tf_op jit(solution)/shard_map/fit/pallas_call | solution.py:310
Async XLA Ops:
  2.2 16.7 %all-to-all-start = ((f32[16,16,128]{2,1,0:T(8,128)}), f32[16,16,128]{2,1,0:T(8,128)S(1)}, u32[]{:S(2)}, u32[]{:S(2)}) async-start(f32[16,16,128]{2,1,0:T(8,128)} %get-tuple-element.19), calls=%async_computation | async-start | bytes 262144 | tf_op jit(solution)/shard_map/all_to_all | solution.py:335
  9.6 7.8 %collective-permute-start = (f32[80,128]{1,0:T(8,128)S(1)}, f32[80,128]{1,0:T(8,128)S(1)}, u32[]{:S(2)}, u32[]{:S(2)}) collective-permute-start(f32[80,128]{1,0:T(8,128)S(1)} %get-tuple-element.13.far), channel_id=1, source_target_pairs={{16,32},{48,64},{80,96},{112,128},{144,160},{176,192},{208,224},{2... | collective-permute-start | bytes 122888 | tf_op jit(solution)/shard_map/ppermute | solution.py:337
  15.4 3.1 %collective-permute-start.1 = (f32[80,128]{1,0:T(8,128)S(1)}, f32[80,128]{1,0:T(8,128)S(1)}, u32[]{:S(2)}, u32[]{:S(2)}) collective-permute-start(f32[80,128]{1,0:T(8,128)S(1)} %get-tuple-element.14.near), channel_id=1, source_target_pairs={{0,16},{32,48},{64,80},{96,112},{128,144},{160,176},{192,208},{224... | collective-permute-start | bytes 122888 | tf_op jit(solution)/shard_map/ppermute | solution.py:338

commit v6 on v5

--- a/solution.py
+++ b/solution.py
@@ -182,7 +182,7 @@
     acc_c, acc_t = accs[:NS], accs[NS:]
     row16 = lax.broadcasted_iota(jnp.int32, (SUB, LANES), 0)
     NT = lc.shape[0]
-    KC = 256
+    KC = 2 * R
     n1 = NT // KC
     G = KC // R
     NG = NT // R
@@ -200,11 +200,14 @@
             dst[pl.ds(s * LANES, LANES), :] = st.T.astype(BF)
         cc = (2.0 * blk + 1.0) * (1.0 / 128.0)
         cc = jnp.where(row16 == 13, 1.0, jnp.where((row16 >= 10) & (row16 < 13), cc, 0.0))
-        cs[:, pl.ds(s * LANES, LANES)] = cc.astype(BF)
+        cc = cc.astype(BF)
+        for h in range(2):
+            half = cc[:, h * R : h * R + R]
+            cs[:, pl.ds((2 * s + h) * LANES, LANES)] = jnp.concatenate([half, half], axis=1)
 
     def push(i, tile, stage):
         for mxu, side in enumerate((fc_ref, ft_ref)):
-            e = ze if tile is None else e_ref[pl.ds(tile * KC + mxu * LANES, LANES), :]
+            e = ze if tile is None else e_ref[pl.ds((2 * tile + mxu) * LANES, LANES), :]
             pltpu.matmul_push_rhs(jnp.concatenate([side[i], e], axis=0), stage, mxu)
 
     def issue(q, stage):
@@ -213,7 +216,7 @@
 
     def edot(tile, stage=None):
         for mxu, acc in enumerate((acc_e0, acc_e1)):
-            lhs = jnp.concatenate([zs, cs[:, pl.ds(tile * KC + mxu * LANES, LANES)]], axis=1)
+            lhs = jnp.concatenate([zs, cs[:, pl.ds((2 * tile + mxu) * LANES, LANES)]], axis=1)
             pltpu.matmul_acc_lhs(acc, lhs, load_staged_rhs=stage)
 
     def take(q, m):
@@ -226,7 +229,10 @@
 
     def exps(q, m):
         rows = pl.ds(q * R, R)
-        e_ref[rows, :] = jnp.exp2(g_ref[rows, :] - m).astype(BF)
+        e = jnp.exp2(g_ref[rows, :] - m)
+        hi = e.astype(BF)
+        e_ref[pl.ds(q * LANES, R), :] = hi
+        e_ref[pl.ds(q * LANES + R, R), :] = (e - hi.astype(F32)).astype(BF)
 
     def finish(r2, m):
         acc = pltpu.matmul_pop(acc_e0) + pltpu.matmul_pop(acc_e1)
@@ -243,7 +249,7 @@
     top = lambda m: jnp.max(m, axis=0, keepdims=True)
     last = 7
     g_ref[pl.ds((NG - L) * R, L * R), :] = jnp.zeros((L * R, 256), F32)
-    e_ref[pl.ds((n1 - S) * KC, S * KC), :] = jnp.ones((S * KC, 256), BF)
+    e_ref[pl.ds((n1 - S) * 2 * LANES, S * 2 * LANES), :] = jnp.ones((S * 2 * LANES, 256), BF)
 
     push(0, None, 0)
     m = None
@@ -304,7 +310,7 @@
     finish(last, new)
 
 
-def fit(fc, ft, ff, bank, R=64, NS=8, L=7, S=3, PR=3):
+def fit(fc, ft, ff, bank, R=64, NS=8, L=7, S=5, PR=1):
     vm = pl.BlockSpec(memory_space=pltpu.VMEM)
     nt = bank.shape[0] * LANES
     return pl.pallas_call(
@@ -315,9 +321,9 @@
         scratch_shapes=[
             pltpu.VMEM((nt, LANES), BF),
             pltpu.VMEM((nt, LANES), BF),
-            pltpu.VMEM((SUB, nt), BF),
+            pltpu.VMEM((SUB, 2 * nt), BF),
             pltpu.VMEM((nt, 256), F32),
-            pltpu.VMEM((nt, 256), BF),
+            pltpu.VMEM((2 * nt, 256), BF),
         ],
         name="fit",
     )(on_chip(fc), on_chip(ft), on_chip(ff), on_chip(bank))

time: 25.9 us -> 27.5 us (1.062)
  the two profiles are of different devices: /device:TPU:99 before, /device:TPU:227 now
where the time goes in v6:
time: 27.5 us; the launch traced here: 27.2 us
  starting transfers between devices  14.7 us (53%)
  Pallas kernels  10.6 us (39%)
  waiting for transfers between devices  1.18 us (4%)
  between operations  0.68 us (2%)
    pallas_call x1, Pallas kernels, fit(): pl.pallas_call(functools.partial(fit_kernel, R=R, L=L, NS=NS, S=S, PR=PR)...  8.29 us
    all_to_all x1, starting transfers between devices, body(): bank = lax.all_to_all(bank, 'tmpl', split_axis=0, concat_axis=0, tiled=True)  6.93 us
    ppermute x1, starting transfers between devices, body(): got_far = lax.ppermute(far, 'tile', swaps(1, tiles))  5.88 us
    ppermute x1, starting transfers between devices, body(): got_near = lax.ppermute(near, 'tile', swaps(0, tiles))  1.92 us
    pallas_call x1, Pallas kernels, head(): pl.pallas_call(head_kernel, out_shape=(jax.ShapeDtypeStruct((shards, SUB,...  1.57 us
    ppermute x1, waiting for transfers between devices, body(): got_near = lax.ppermute(near, 'tile', swaps(0, tiles))  1.17 us
  transfers between devices with their start and end apart: 3, of which 1 were waited for; matrix products, arithmetic and copies ran while one was open for 0% of the time, Pallas kernels for 3%

profile of v6, /device:TPU:227, one launch (start us, length us, event | category | flops | bytes accessed | tf_op | source)
XLA Modules:
  0.0 27.2 jit_solution(8612436863493794986)
XLA Ops:
  0.6 1.6 %head.1 = (f32[16,16,128]{2,1,0:T(8,128)}, f32[3,10,16,128]{3,2,1,0:T(8,128)S(1)}, f32[10,16,128]{2,1,0:T(8,128)S(1)}, f32[17,16,128]{2,1,0:T(8,128)S(1)}) custom-call(f32[10,16,2048]{2,1,0:T(8,128)} %sky.1, f32[10,16,2048]{2,1,0:T(8,128)} %ivar.1, f32[10,17]{1,0:T(8,128)} %taps.1, s32[10]{0:T(128)} %sizes.1, f32[10,128]{1,0:T(8,128)} %templates.1, ...), custom_call_target="tpu_custom_call" | custom-call | tf_op jit(solution)/shard_map/head/pallas_call | solution.py:68
  2.2 6.9 %all-to-all-start = ((f32[16,16,128]{2,1,0:T(8,128)}), f32[16,16,128]{2,1,0:T(8,128)S(1)}, u32[]{:S(2)}, u32[]{:S(2)}) async-start(f32[16,16,128]{2,1,0:T(8,128)} %get-tuple-element.19), calls=%async_computation | async-start | bytes 262144 | tf_op jit(solution)/shard_map/all_to_all | solution.py:341
  9.1 0.4 %columns.1 = (f32[80,128]{1,0:T(8,128)S(1)}, f32[80,128]{1,0:T(8,128)S(1)}) custom-call(f32[3,10,16,128]{3,2,1,0:T(8,128)S(1)} %get-tuple-element.11.cols, f32[17,16,128]{2,1,0:T(8,128)S(1)} %get-tuple-element.12.kv), custom_call_target="tpu_custom_call" | custom-call | tf_op jit(solution)/shard_map/columns/pallas_call | solution.py:117
  9.6 5.9 %collective-permute-start = (f32[80,128]{1,0:T(8,128)S(1)}, f32[80,128]{1,0:T(8,128)S(1)}, u32[]{:S(2)}, u32[]{:S(2)}) collective-permute-start(f32[80,128]{1,0:T(8,128)S(1)} %get-tuple-element.13.far), channel_id=1, source_target_pairs={{16,32},{48,64},{80,96},{112,128},{144,160},{176,192},{208,224},{2... | collective-permute-start | bytes 122888 | tf_op jit(solution)/shard_map/ppermute | solution.py:343
  15.4 1.9 %collective-permute-start.1 = (f32[80,128]{1,0:T(8,128)S(1)}, f32[80,128]{1,0:T(8,128)S(1)}, u32[]{:S(2)}, u32[]{:S(2)}) collective-permute-start(f32[80,128]{1,0:T(8,128)S(1)} %get-tuple-element.14.near), channel_id=1, source_target_pairs={{0,16},{32,48},{64,80},{96,112},{128,144},{160,176},{192,208},{224... | collective-permute-start | bytes 122888 | tf_op jit(solution)/shard_map/ppermute | solution.py:344
  17.4 0.0 collective-permute-done.got_far
  17.4 1.2 %collective-permute-done.1.got_near = f32[80,128]{1,0:T(8,128)S(1)} collective-permute-done((f32[80,128]{1,0:T(8,128)S(1)}, f32[80,128]{1,0:T(8,128)S(1)}, u32[]{:S(2)}, u32[]{:S(2)}) %collective-permute-start.1) | collective-permute-done | bytes 40992 | tf_op jit(solution)/shard_map/ppermute | solution.py:344
  18.6 0.3 %rows.1 = (bf16[8,128,256]{2,1,0:T(8,128)(2,1)S(1)}, bf16[8,128,256]{2,1,0:T(8,128)(2,1)S(1)}, f32[16,128]{1,0:T(8,128)S(1)}) custom-call(f32[80,128]{1,0:T(8,128)S(1)} %collective-permute-done.got_far, f32[80,128]{1,0:T(8,128)S(1)} %collective-permute-done.1.got_near, f32[80,128]{1,0:T(8,128)S(1)} %get-tuple-element.13.far, ...), custom_call_target="tpu_custom_call" | custom-call | tf_op jit(solution)/shard_map/rows/pallas_call | solution.py:157
  18.9 0.0 all-to-all-done.bank
  18.9 8.3 %fit.1 = (f32[3,16,128]{2,1,0:T(8,128)}, f32[16,128]{1,0:T(8,128)}) custom-call(bf16[8,128,256]{2,1,0:T(8,128)(2,1)S(1)} %get-tuple-element.16.fc_ref, bf16[8,128,256]{2,1,0:T(8,128)(2,1)S(1)} %get-tuple-element.17.ft_ref, f32[16,128]{1,0:T(8,128)S(1)} %get-tuple-element.18.ff_ref, f32[16,16,128]{2,1,0:T(8,128)S(1)} %all-to-all-done.bank), custom_call_target="tpu_custom_call" | custom-call | tf_op jit(solution)/shard_map/fit/pallas_call | solution.py:316
Async XLA Ops:
  2.2 16.7 %all-to-all-start = ((f32[16,16,128]{2,1,0:T(8,128)}), f32[16,16,128]{2,1,0:T(8,128)S(1)}, u32[]{:S(2)}, u32[]{:S(2)}) async-start(f32[16,16,128]{2,1,0:T(8,128)} %get-tuple-element.19), calls=%async_computation | async-start | bytes 262144 | tf_op jit(solution)/shard_map/all_to_all | solution.py:341
  9.6 7.8 %collective-permute-start = (f32[80,128]{1,0:T(8,128)S(1)}, f32[80,128]{1,0:T(8,128)S(1)}, u32[]{:S(2)}, u32[]{:S(2)}) collective-permute-start(f32[80,128]{1,0:T(8,128)S(1)} %get-tuple-element.13.far), channel_id=1, source_target_pairs={{16,32},{48,64},{80,96},{112,128},{144,160},{176,192},{208,224},{2... | collective-permute-start | bytes 122888 | tf_op jit(solution)/shard_map/ppermute | solution.py:343
  15.4 3.1 %collective-permute-start.1 = (f32[80,128]{1,0:T(8,128)S(1)}, f32[80,128]{1,0:T(8,128)S(1)}, u32[]{:S(2)}, u32[]{:S(2)}) collective-permute-start(f32[80,128]{1,0:T(8,128)S(1)} %get-tuple-element.14.near), channel_id=1, source_target_pairs={{0,16},{32,48},{64,80},{96,112},{128,144},{160,176},{192,208},{224... | collective-permute-start | bytes 122888 | tf_op jit(solution)/shard_map/ppermute | solution.py:344
